TPU v7x, 256 devices: a whole 4x4x8 slice. The times are simulated.
256 devices in a mesh: lon: 32 (over z, y_hi, core), lat: 8 (over y_lo, x).
Axes of the slice: x: 4, y: 4 (y_hi: 2, y_lo: 2; y = y_hi * 2 + y_lo), z: 8, core: 2. Of those that a mesh axis runs over, the one named last changes fastest.
Arguments:
- state: bfloat16 [360, 768, 128], P('lat', 'lon'), may hold values from -6 to 6
- land_sea: int32 [360, 768], P('lat', 'lon'), may hold values 0 or 1
- cotangent: bfloat16 [360, 768, 128], P('lat', 'lon'), may hold values from -6 to 6
- dw_kernel: bfloat16 [2, 7, 7, 128], replicated, may hold values from -0.875 to 0.875
- conv_bias: float32 [2, 128], replicated, may hold values from -3 to 3
- norm_gain: float32 [2, 128], replicated, may hold values from 0.1 to 1.9
- norm_bias: float32 [2, 128], replicated, may hold values from -3 to 3
- weight_in: bfloat16 [2, 128, 512], replicated, may hold values from -0.5 to 0.5
- bias_in: float32 [2, 512], replicated, may hold values from -3 to 3
- weight_out: bfloat16 [2, 512, 128], replicated, may hold values from -0.25 to 0.25
- bias_out: float32 [2, 128], replicated, may hold values from -3 to 3
- layer_scale: float32 [2, 128], replicated, may hold values from 0.3 to 1
Outputs:
- output: bfloat16 [360, 768, 128], P('lat', 'lon')
- grad_state: bfloat16 [360, 768, 128], P('lat', 'lon')
- grad_dw_kernel: float32 [2, 7, 7, 128], replicated
- grad_conv_bias: float32 [2, 128], replicated
- grad_norm_gain: float32 [2, 128], replicated
- grad_norm_bias: float32 [2, 128], replicated
- grad_weight_in: float32 [2, 128, 512], replicated
- grad_bias_in: float32 [2, 512], replicated
- grad_weight_out: float32 [2, 512, 128], replicated
- grad_bias_out: float32 [2, 128], replicated
- grad_layer_scale: float32 [2, 128], replicated
All inputs are finite; a program needn't handle non-finite values. No bound on the sum of `land_sea` on one device may be relied on, other than what follows from the above.
Results may differ from a plain program's by a relative error of at most 0.02.
Values may be sent and summed in bfloat16 or wider, within the bound.
A program may use at most 64 MiB of HBM per device.

v0:
```python
import math

import jax
import jax.numpy as jnp
from jax import lax
from jax.experimental import pallas as pl
from jax.experimental.pallas import tpu as pltpu
from jax.sharding import PartitionSpec as P

KSIZE = 7
BLOCKS = 2
C = 128
F = 512
EPS_NORM = 1e-06
INV_ROOT_TWO = 0.7071067811865476
INV_ROOT_TWO_PI = 0.3989422804014327
MESH_ID = pl.DeviceIdType.MESH
GROUP = 16
ROWS = 45
COLS = 24
MARGIN = 3
AROUND = ((1, 0), (-1, 0), (0, 1), (0, -1), (1, 1), (1, -1), (-1, 1), (-1, -1))
STRIP = 9
CHUNKS = ROWS // STRIP
CELLS = STRIP * COLS


def position():
    lon = lax.axis_index("lon")
    lat = lax.axis_index("lat")
    z = lon // 4
    y_hi = lax.rem(lon // 2, 2)
    core = lax.rem(lon, 2)
    plane = y_hi * 8 + lat
    line = z * 2 + core
    return plane, line


def plane_peer(plane, line):
    lon = (line // 2) * 4 + (plane // 8) * 2 + lax.rem(line, 2)
    return {"lon": lon, "lat": lax.rem(plane, 8)}


def beside(east, south):
    return {
        "lon": lax.rem(lax.axis_index("lon") + east + 32, 32),
        "lat": lax.rem(lax.axis_index("lat") + south + 8, 8),
    }


def greet(barrier):
    plane, line = position()

    def one(k, carry):
        other = lax.rem(plane + k, GROUP)
        pl.semaphore_signal(
            barrier, inc=1, device_id=plane_peer(other, line), device_id_type=MESH_ID
        )
        other = lax.rem(line + k, GROUP)
        pl.semaphore_signal(
            barrier, inc=1, device_id=plane_peer(plane, other), device_id_type=MESH_ID
        )
        return carry

    lax.fori_loop(1, GROUP, one, 0)
    for east, south in AROUND:
        pl.semaphore_signal(
            barrier, inc=1, device_id=beside(east, south), device_id_type=MESH_ID
        )
    pl.semaphore_wait(barrier, 2 * (GROUP - 1) + len(AROUND))


class Exchange:
    def __init__(self, kind, scatter, src, dst, send, recv):
        self.plane, self.line = position()
        self.kind = kind
        self.scatter = scatter
        self.src, self.dst, self.send, self.recv = src, dst, send, recv
        self.me = self.plane if kind == "plane" else self.line

    def copy(self, k):
        other = lax.rem(self.me + k, GROUP)
        if self.kind == "plane":
            target = plane_peer(other, self.line)
        else:
            target = plane_peer(self.plane, other)
        src = self.src.at[other] if self.scatter else self.src
        return pltpu.make_async_remote_copy(
            src_ref=src,
            dst_ref=self.dst.at[k],
            send_sem=self.send.at[k],
            recv_sem=self.recv.at[k],
            device_id=target,
            device_id_type=MESH_ID,
        )

    def start(self):
        def one(k, carry):
            self.copy(k).start()
            return carry

        lax.fori_loop(1, GROUP, one, 0)

    def wait(self):
        def one(k, carry):
            self.copy(k).wait()
            return carry

        lax.fori_loop(1, GROUP, one, 0)


def slot_sum(own, slots, count=GROUP):
    def one(k, total):
        return total + slots[k].astype(jnp.float32)

    return lax.fori_loop(1, count, one, own)


def f32(value):
    return value.astype(jnp.float32)


def bf16(value):
    return value.astype(jnp.bfloat16)


class Halo:
    def __init__(self, bufs, sems, index, window):
        east, west, north, south, from_west, from_east, from_north, from_south = (
            ref.at[index] for ref in bufs
        )
        self.bufs = (east, west, north, south, from_west, from_east, from_north, from_south)
        self.window = window
        last = ROWS - MARGIN
        tall = pl.ds(MARGIN, ROWS)
        above, below = pl.ds(0, MARGIN), pl.ds(MARGIN + ROWS, MARGIN)
        top, bottom = pl.ds(0, MARGIN), pl.ds(last, MARGIN)
        pairs = (
            (east, from_west.at[tall]),
            (west, from_east.at[tall]),
            (south, from_north),
            (north, from_south),
            (east.at[bottom], from_west.at[above]),
            (east.at[top], from_west.at[below]),
            (west.at[bottom], from_east.at[above]),
            (west.at[top], from_east.at[below]),
        )
        self.copies = [
            pltpu.make_async_remote_copy(
                src_ref=pair[0],
                dst_ref=pair[1],
                send_sem=sems.at[index, 0, k],
                recv_sem=sems.at[index, 1, k],
                device_id=beside(*AROUND[k]),
                device_id_type=MESH_ID,
            )
            for k, pair in enumerate(pairs)
        ]

    def start(self):
        east, west, north, south = self.bufs[:4]
        window = self.window
        inner = slice(MARGIN, MARGIN + ROWS)
        east[...] = bf16(window[inner, COLS : COLS + MARGIN, :])
        west[...] = bf16(window[inner, MARGIN : 2 * MARGIN, :])
        north[...] = bf16(window[MARGIN : 2 * MARGIN, MARGIN : MARGIN + COLS, :])
        south[...] = bf16(window[ROWS : ROWS + MARGIN, MARGIN : MARGIN + COLS, :])
        for copy in self.copies:
            copy.start()

    def finish(self):
        for copy in self.copies:
            copy.wait()
        from_west, from_east, from_north, from_south = self.bufs[4:]
        lat = lax.axis_index("lat")
        has_north = jnp.where(lat > 0, 1.0, 0.0).astype(jnp.float32)
        has_south = jnp.where(lat < 7, 1.0, 0.0).astype(jnp.float32)
        window = self.window
        inner = slice(MARGIN, MARGIN + ROWS)
        above, below = slice(0, MARGIN), slice(MARGIN + ROWS, 2 * MARGIN + ROWS)
        middle = slice(MARGIN, MARGIN + COLS)
        window[above, middle, :] = f32(from_north[...]) * has_north
        window[below, middle, :] = f32(from_south[...]) * has_south
        for ref, side in (
            (from_west, slice(0, MARGIN)),
            (from_east, slice(MARGIN + COLS, 2 * MARGIN + COLS)),
        ):
            window[inner, side, :] = f32(ref[inner])
            window[above, side, :] = f32(ref[above]) * has_north
            window[below, side, :] = f32(ref[below]) * has_south


def convolve(window, weight, first, flip):
    def rows(base):
        sums = first(base)
        for i in range(KSIZE + 2):
            for b in range(KSIZE):
                piece = window[base + i, b : b + COLS, :]
                for o in range(3):
                    a = i - o
                    if 0 <= a < KSIZE:
                        tap = weight(KSIZE - 1 - a, KSIZE - 1 - b) if flip else weight(a, b)
                        sums[o] = sums[o] + piece * tap
        return sums

    return rows


def fold(value):
    return jnp.sum(value.reshape(value.shape[0] // 8, 8, value.shape[1]), axis=0)


def lane_mean(value):
    return jnp.mean(value, axis=-1, keepdims=True)


def step_kernel(
    grad_norm,
    state,
    land_sea,
    cotangent,
    dw_kernel,
    conv_bias,
    norm_gain,
    norm_bias,
    weight_in,
    bias_in,
    weight_out,
    bias_out,
    layer_scale,
    out,
    grad_state,
    g_kernel,
    g_conv,
    g_gain,
    g_shift,
    g_win,
    g_bias_in,
    g_wout,
    g_bias_out,
    g_scale,
    win1,
    win2,
    gwin1,
    gwin2,
    taps,
    mask,
    mixed,
    hidden,
    active,
    slope,
    normed,
    inverse,
    branch,
    upstream,
    acc_win,
    acc_wout,
    acc_rows,
    acc_bias,
    acc_taps,
    h_east,
    h_west,
    h_north,
    h_south,
    h_from_west,
    h_from_east,
    h_from_north,
    h_from_south,
    sem_h,
    small,
    send_a,
    recv_a,
    send_b,
    recv_b,
    own_b,
    back_b,
    own_a,
    back_a,
    srecv_a,
    sown_b,
    srecv_b,
    sown_a,
    sback_a,
    sem_w,
    sem_s,
):
    plane, line = position()
    greet(pltpu.get_barrier_semaphore())
    halo_bufs = (
        h_east, h_west, h_north, h_south, h_from_west, h_from_east, h_from_north, h_from_south
    )
    middle = slice(MARGIN, MARGIN + COLS)

    def widen(c, carry):
        win1[pl.ds(MARGIN + c * STRIP, STRIP), middle, :] = f32(state[pl.ds(c * STRIP, STRIP)])
        return carry

    lax.fori_loop(0, CHUNKS, widen, 0)
    halo = Halo(halo_bufs, sem_h, 0, win1)
    halo.start()

    for blk in range(BLOCKS):
        for a in range(KSIZE):
            taps[blk, a, 0:KSIZE, :] = f32(dw_kernel[blk, a])
    eye = lax.broadcasted_iota(jnp.int32, (COLS, COLS), 0) == lax.broadcasted_iota(
        jnp.int32, (COLS, COLS), 1
    )
    ones = jnp.ones((COLS, C), jnp.float32)

    def spread(i, carry):
        row = jnp.broadcast_to(land_sea[pl.ds(i, 1), :].astype(jnp.float32), (COLS, COLS))
        mask[i] = jnp.dot(
            jnp.where(eye, row, 0.0), ones, preferred_element_type=jnp.float32
        )
        return carry

    lax.fori_loop(0, ROWS, spread, 0)
    acc_win[...] = jnp.zeros_like(acc_win)
    acc_wout[...] = jnp.zeros_like(acc_wout)
    acc_rows[...] = jnp.zeros_like(acc_rows)
    acc_bias[...] = jnp.zeros_like(acc_bias)
    acc_taps[...] = jnp.zeros_like(acc_taps)

    def mix(window, blk):
        start = jnp.broadcast_to(conv_bias[blk : blk + 1, :], (COLS, C))
        rows = convolve(
            window, lambda a, b: taps[blk, a, b : b + 1, :], lambda base: [start] * 3, False
        )

        def three(g, carry):
            sums = rows(g * 3)
            for o in range(3):
                mixed[g * 3 + o] = sums[o]
            return carry

        lax.fori_loop(0, ROWS // 3, three, 0)

    def forward(c, window, blk, keep):
        x = mixed[pl.ds(c * STRIP, STRIP)].reshape(CELLS, C)
        center = x - lane_mean(x)
        inv = lax.rsqrt(lane_mean(center * center) + EPS_NORM)
        norm = center * inv
        normed[keep] = norm
        inverse[keep] = jnp.broadcast_to(inv, (CELLS, C))
        lifted = bf16(norm * norm_gain[blk : blk + 1, :] + norm_bias[blk : blk + 1, :])
        hidden[...] = jnp.dot(lifted, weight_in[blk], preferred_element_type=jnp.float32)

        def gelu(t, carry):
            rows = pl.ds(pl.multiple_of(t * COLS, 8), COLS)
            h = hidden[rows, :] + bias_in[blk : blk + 1, :]
            cumulative = 0.5 * (1.0 + lax.erf(h * INV_ROOT_TWO))
            density = jnp.exp(-0.5 * h * h) * INV_ROOT_TWO_PI
            active[keep, rows, :] = h * cumulative
            slope[keep, rows, :] = cumulative + h * density
            return carry

        lax.fori_loop(0, STRIP, gelu, 0)
        act = bf16(active[keep])
        branch_c = (
            jnp.dot(act, weight_out[blk], preferred_element_type=jnp.float32)
            + bias_out[blk : blk + 1, :]
        )
        branch[keep] = branch_c
        inner = window[pl.ds(MARGIN + c * STRIP, STRIP), middle, :].reshape(CELLS, C)
        ocean = mask[pl.ds(c * STRIP, STRIP)].reshape(CELLS, C)
        return (inner + layer_scale[blk : blk + 1, :] * branch_c) * ocean

    def backward(c, incoming, gwindow, blk, keep):
        ocean = mask[pl.ds(c * STRIP, STRIP)].reshape(CELLS, C)
        masked = incoming * ocean
        upstream[pl.ds(c * STRIP, STRIP)] = masked.reshape(STRIP, COLS, C)
        gb = bf16(masked * layer_scale[blk : blk + 1, :])
        acc_rows[blk, 4] += fold(masked * branch[keep])
        acc_rows[blk, 3] += fold(f32(gb))
        rows_rows = (((0,), (0,)), ((), ()))
        cols_cols = (((1,), (1,)), ((), ()))
        acc_wout[blk] += lax.dot_general(
            gb, bf16(active[keep]), rows_rows, preferred_element_type=jnp.float32
        )
        hidden[...] = lax.dot_general(
            gb, weight_out[blk], cols_cols, preferred_element_type=jnp.float32
        )

        def through(t, total):
            rows = pl.ds(pl.multiple_of(t * COLS, 8), COLS)
            gh = f32(bf16(hidden[rows, :] * slope[keep, rows, :]))
            hidden[rows, :] = gh
            return total + fold(gh)

        acc_bias[blk] = lax.fori_loop(0, STRIP, through, acc_bias[blk])
        gh = bf16(hidden[...])
        norm = normed[keep]
        gain = norm_gain[blk : blk + 1, :]
        lifted = bf16(norm * gain + norm_bias[blk : blk + 1, :])
        acc_win[blk] += lax.dot_general(
            lifted, gh, rows_rows, preferred_element_type=jnp.float32
        )
        gl = lax.dot_general(gh, weight_in[blk], cols_cols, preferred_element_type=jnp.float32)
        acc_rows[blk, 1] += fold(gl * norm)
        acc_rows[blk, 2] += fold(gl)
        s = gl * gain
        gm = inverse[keep] * (s - lane_mean(s) - norm * lane_mean(s * norm))
        gm = f32(bf16(gm))
        acc_rows[blk, 0] += fold(gm)
        gwindow[pl.ds(MARGIN + c * STRIP, STRIP), middle, :] = gm.reshape(STRIP, COLS, C)

    def tap_sums(window, gwindow, blk):
        def three(g, carry):
            base = g * 3
            grads = [gwindow[base + MARGIN + o, middle, :] for o in range(3)]
            for b in range(KSIZE):
                parts = [None] * KSIZE
                for i in range(KSIZE + 2):
                    piece = window[base + i, b : b + COLS, :]
                    for o in range(3):
                        a = i - o
                        if 0 <= a < KSIZE:
                            term = piece * grads[o]
                            parts[a] = term if parts[a] is None else parts[a] + term
                for a in range(KSIZE):
                    acc_taps[blk, a * KSIZE + b] += fold(parts[a])
            return carry

        lax.fori_loop(0, ROWS // 3, three, 0)

    def adjoint(gwindow, blk, put):
        rows = convolve(
            gwindow,
            lambda a, b: taps[blk, a, b : b + 1, :],
            lambda base: [upstream[base + o] for o in range(3)],
            True,
        )

        def three(g, carry):
            sums = rows(g * 3)
            for o in range(3):
                put(g * 3 + o, sums[o])
            return carry

        lax.fori_loop(0, ROWS // 3, three, 0)

    def scatter_weights(blk):
        for q in range(4):
            for half in range(2):
                send_a[blk, 2 * q + half] = bf16(
                    acc_win[blk, half * 64 : half * 64 + 64, q * 128 : q * 128 + 128]
                )
            turned = jnp.transpose(acc_wout[blk, :, q * 128 : q * 128 + 128])
            for half in range(2):
                send_a[blk, 8 + 2 * q + half] = bf16(turned[half * 64 : half * 64 + 64])
        ex = Exchange(
            "plane", True, send_a.at[blk], recv_a.at[blk], sem_w.at[blk, 0], sem_w.at[blk, 1]
        )
        ex.start()
        return ex

    def line_scatter(ex, blk):
        ex.wait()
        total = slot_sum(f32(send_a[blk, plane]), recv_a.at[blk])
        for j in range(GROUP):
            send_b[blk, j] = total[j * 4 : j * 4 + 4]
        ex = Exchange(
            "line", True, send_b.at[blk], recv_b.at[blk], sem_w.at[blk, 2], sem_w.at[blk, 3]
        )
        ex.start()
        return ex

    def line_gather(ex, blk):
        ex.wait()
        own_b[blk] = slot_sum(send_b[blk, line], recv_b.at[blk])
        ex = Exchange(
            "line", False, own_b.at[blk], back_b.at[blk], sem_w.at[blk, 4], sem_w.at[blk, 5]
        )
        ex.start()
        return ex

    def plane_gather(ex, blk):
        ex.wait()
        back_b[blk, 0] = own_b[blk]
        for j in range(GROUP):
            sub = back_b[blk, lax.rem(line - j + GROUP, GROUP)]
            own_a[blk, j * 4 : j * 4 + 4] = bf16(sub)
        ex = Exchange(
            "plane", False, own_a.at[blk], back_a.at[blk], sem_w.at[blk, 6], sem_w.at[blk, 7]
        )
        ex.start()
        return ex

    def finish_weights(ex, blk):
        ex.wait()
        back_a[blk, 0] = own_a[blk]
        for p in range(GROUP):
            piece = f32(back_a[blk, lax.rem(plane - p + GROUP, GROUP)]) * grad_norm
            if p < 8:
                g_win[
                    blk, (p % 2) * 64 : (p % 2) * 64 + 64, (p // 2) * 128 : (p // 2) * 128 + 128
                ] = piece
            else:
                g_wout[blk, (p - 8) * 64 : (p - 8) * 64 + 64] = piece

    def small_row(blk, r, value):
        i = blk * 4 + r % 4
        small[r // 4, i : i + 1, :] = jnp.sum(value, axis=0, keepdims=True)

    def pack_rows(blk):
        for tap in range(KSIZE * KSIZE):
            small_row(blk, tap, acc_taps[blk, tap])
        for k in range(5):
            small_row(blk, 49 + k, acc_rows[blk, k])
        for q in range(4):
            small_row(blk, 54 + q, acc_bias[blk, :, q * 128 : q * 128 + 128])

    halo.finish()
    mix(win1, 0)

    def forward_one(c, carry):
        result = forward(c, win1, 0, c)
        win2[pl.ds(MARGIN + c * STRIP, STRIP), middle, :] = f32(bf16(result)).reshape(
            STRIP, COLS, C
        )
        return carry

    lax.fori_loop(0, CHUNKS, forward_one, 0)
    halo = Halo(halo_bufs, sem_h, 1, win2)
    halo.start()
    small[...] = jnp.zeros_like(small)
    halo.finish()
    mix(win2, 1)

    def both(c, carry):
        result = forward(c, win2, 1, CHUNKS)
        out[pl.ds(c * STRIP, STRIP)] = bf16(result.reshape(STRIP, COLS, C))
        incoming = f32(cotangent[pl.ds(c * STRIP, STRIP)]).reshape(CELLS, C)
        backward(c, incoming, gwin2, 1, CHUNKS)
        return carry

    lax.fori_loop(0, CHUNKS, both, 0)
    halo = Halo(halo_bufs, sem_h, 2, gwin2)
    halo.start()
    second = scatter_weights(1)
    tap_sums(win2, gwin2, 1)
    halo.finish()

    def put_mixed(row, value):
        mixed[row] = f32(bf16(value))

    adjoint(gwin2, 1, put_mixed)
    second = line_scatter(second, 1)

    def backward_one(c, carry):
        incoming = mixed[pl.ds(c * STRIP, STRIP)].reshape(CELLS, C)
        backward(c, incoming, gwin1, 0, c)
        return carry

    lax.fori_loop(0, CHUNKS, backward_one, 0)
    halo = Halo(halo_bufs, sem_h, 3, gwin1)
    halo.start()
    first = scatter_weights(0)
    second = line_gather(second, 1)
    tap_sums(win1, gwin1, 0)
    pack_rows(1)
    pack_rows(0)
    tiny = Exchange("plane", True, small, srecv_a, sem_s.at[0], sem_s.at[1])
    tiny.start()
    first = line_scatter(first, 0)
    halo.finish()

    def put_state(row, value):
        grad_state[row] = bf16(value)

    adjoint(gwin1, 0, put_state)
    first = line_gather(first, 0)
    tiny.wait()
    sown_b[...] = slot_sum(small[plane], srecv_a)
    tiny = Exchange("line", False, sown_b, srecv_b, sem_s.at[2], sem_s.at[3])
    tiny.start()
    second = plane_gather(second, 1)
    first = plane_gather(first, 0)
    tiny.wait()
    sown_a[...] = slot_sum(sown_b[...], srecv_b)
    tiny = Exchange("plane", False, sown_a, sback_a, sem_s.at[4], sem_s.at[5])
    tiny.start()
    finish_weights(second, 1)
    finish_weights(first, 0)
    tiny.wait()
    sback_a[0] = sown_a[...]
    for p in range(GROUP):
        small[p] = sback_a[lax.rem(plane - p + GROUP, GROUP)] * grad_norm
    for blk in range(BLOCKS):

        def row_of(r):
            return small[r // 4, blk * 4 + r % 4 : blk * 4 + r % 4 + 1, :]

        for a in range(KSIZE):
            for b in range(KSIZE):
                g_kernel[blk, a, b : b + 1, :] = row_of(a * KSIZE + b)
        for k, ref in enumerate((g_conv, g_gain, g_shift, g_bias_out, g_scale)):
            ref[blk : blk + 1, :] = row_of(49 + k)
        for q in range(4):
            g_bias_in[blk : blk + 1, q * 128 : q * 128 + 128] = row_of(54 + q)


def on_device(*arrays):
    vmem = pl.BlockSpec(memory_space=pltpu.VMEM)
    grad_norm = 1.0 / math.sqrt(
        lax.axis_size("lat") * ROWS * lax.axis_size("lon") * COLS
    )
    field = jax.ShapeDtypeStruct((ROWS, COLS, C), jnp.bfloat16)
    row = jax.ShapeDtypeStruct((BLOCKS, C), jnp.float32)

    def vm(*shape, dtype=jnp.float32):
        return pltpu.VMEM(shape, dtype)

    tall, wide = ROWS + 2 * MARGIN, COLS + 8
    half = jnp.bfloat16
    return pl.pallas_call(
        lambda *refs: step_kernel(grad_norm, *refs),
        name="ocean_step",
        out_shape=(
            field,
            field,
            jax.ShapeDtypeStruct((BLOCKS, KSIZE, KSIZE, C), jnp.float32),
            row,
            row,
            row,
            jax.ShapeDtypeStruct((BLOCKS, C, F), jnp.float32),
            jax.ShapeDtypeStruct((BLOCKS, F), jnp.float32),
            jax.ShapeDtypeStruct((BLOCKS, F, C), jnp.float32),
            row,
            row,
        ),
        in_specs=[vmem] * 12,
        out_specs=(vmem,) * 11,
        scratch_shapes=[
            vm(tall, wide, C),
            vm(tall, wide, C),
            vm(tall, wide, C),
            vm(tall, wide, C),
            vm(BLOCKS, KSIZE, 8, C),
            vm(ROWS, COLS, C),
            vm(ROWS, COLS, C),
            vm(CELLS, F),
            vm(CHUNKS + 1, CELLS, F),
            vm(CHUNKS + 1, CELLS, F),
            vm(CHUNKS + 1, CELLS, C),
            vm(CHUNKS + 1, CELLS, C),
            vm(CHUNKS + 1, CELLS, C),
            vm(ROWS, COLS, C),
            vm(BLOCKS, C, F),
            vm(BLOCKS, C, F),
            vm(BLOCKS, 5, 8, C),
            vm(BLOCKS, 8, F),
            vm(BLOCKS, KSIZE * KSIZE, 8, C),
            vm(4, ROWS, MARGIN, C, dtype=half),
            vm(4, ROWS, MARGIN, C, dtype=half),
            vm(4, MARGIN, COLS, C, dtype=half),
            vm(4, MARGIN, COLS, C, dtype=half),
            vm(4, tall, MARGIN, C, dtype=half),
            vm(4, tall, MARGIN, C, dtype=half),
            vm(4, MARGIN, COLS, C, dtype=half),
            vm(4, MARGIN, COLS, C, dtype=half),
            pltpu.SemaphoreType.DMA((4, 2, len(AROUND))),
            vm(GROUP, 8, C),
            vm(BLOCKS, GROUP, 64, C, dtype=half),
            vm(BLOCKS, GROUP, 64, C, dtype=half),
            vm(BLOCKS, GROUP, 4, C),
            vm(BLOCKS, GROUP, 4, C),
            vm(BLOCKS, 4, C),
            vm(BLOCKS, GROUP, 4, C),
            vm(BLOCKS, 64, C, dtype=half),
            vm(BLOCKS, GROUP, 64, C, dtype=half),
            vm(GROUP, 8, C),
            vm(8, C),
            vm(GROUP, 8, C),
            vm(8, C),
            vm(GROUP, 8, C),
            pltpu.SemaphoreType.DMA((BLOCKS, 8, GROUP)),
            pltpu.SemaphoreType.DMA((6, GROUP)),
        ],
        compiler_params=pltpu.CompilerParams(
            collective_id=0, has_side_effects=True, vmem_limit_bytes=56 << 20
        ),
    )(*arrays)


def solution(mesh):
    field = P("lat", "lon", None)
    return jax.shard_map(
        on_device,
        mesh=mesh,
        in_specs=(field, P("lat", "lon"), field) + (P(),) * 9,
        out_specs=(field, field) + (P(),) * 9,
        check_vma=False,
    )
```

profile of v0, /device:TPU:1, one launch (start us, length us, event | category | flops | bytes accessed | tf_op | source)
XLA Modules:
  0.0 92.8 jit_solution(12176238459114876990)
XLA Ops:
  0.6 0.0 copy-start.3
  0.7 1.4 %copy.23.refs_1_ = s32[45,24]{1,0:T(8,128)} copy(s32[45,24]{0,1:T(8,128)} %param.13) | data formatting | bytes 8640 | tf_op args[1]
  2.1 0.0 copy-done.3
  2.1 0.6 copy.24.refs_3_
  2.7 80.9 %ocean_step.1 = (bf16[45,24,128]{2,1,0:T(8,128)(2,1)}, bf16[45,24,128]{2,1,0:T(8,128)(2,1)}, f32[2,7,7,128]{3,2,1,0:T(8,128)}, f32[2,128]{1,0:T(2,128)}, f32[2,1...) custom-call(bf16[45,24,128]{2,1,0:T(8,128)(2,1)} %refs_0_.1, ...), custom_call_target="tpu_custom_call" | custom-call | tf_op jit(solution)/shard_map/ocean_step/pallas_call | solution.py:616
  83.5 0.0 copy-start.2
  83.5 1.5 %copy.25 = f32[2,7,7,128]{3,0,2,1:T(2,128)} copy(f32[2,7,7,128]{3,2,1,0:T(8,128)} %get-tuple-element.13) | data formatting | bytes 100352 | tf_op jit(solution)/shard_map/ocean_step/pallas_call | solution.py:616
  85.1 1.7 %copy.36 = bf16[45,24,128]{2,1,0:T(8,128)(2,1)} copy(bf16[45,24,128]{2,1,0:T(8,128)(2,1)} %get-tuple-element.33) | data formatting | bytes 552960
  86.8 0.0 copy-done.2
  86.8 0.7 copy.37
  87.5 0.0 copy-done.9
  87.5 0.6 copy.38
  88.1 0.1 copy-done.8
  88.2 0.6 copy.39
  88.7 0.1 copy-done.7
  88.8 0.6 copy.40
  89.4 0.0 copy-done.1
  89.4 0.8 copy.41
  90.2 0.0 copy-done.4
  90.2 0.6 copy.42
  90.8 0.8 copy.43
  91.6 0.6 copy.44
  92.2 0.1 copy-done.5
  92.3 0.6 copy.45
  (10 shorter events, 0.0 us)
Async XLA Ops:
  0.6 1.4 %copy-start.3 = (bf16[2,7,7,128]{3,0,2,1:T(2,128)(2,1)S(1)}, bf16[2,7,7,128]{3,0,2,1:T(2,128)(2,1)}, u32[]{:S(2)}) copy-start(bf16[2,7,7,128]{3,0,2,1:T(2,128)(2,1)} %param.15) | copy-start | bytes 75268
  83.5 3.3 %copy-start.2 = (bf16[45,24,128]{2,1,0:T(8,128)(2,1)S(1)}, bf16[45,24,128]{2,1,0:T(8,128)(2,1)}, u32[]{:S(2)}) copy-start(bf16[45,24,128]{2,1,0:T(8,128)(2,1)} %get-tuple-element.34) | copy-start | bytes 829444
  85.1 4.4 %copy-start.1 = (f32[2,128,512]{2,1,0:T(8,128)S(1)}, f32[2,128,512]{2,1,0:T(8,128)}, u32[]{:S(2)}) copy-start(f32[2,128,512]{2,1,0:T(8,128)} %get-tuple-element.39) | copy-start | bytes 1572868
  86.8 0.7 copy-start.9
  87.5 0.7 copy-start.8
  88.2 0.7 copy-start.7
  89.4 0.8 copy-start.4
  89.4 1.4 %copy-start = (f32[2,512,128]{2,1,0:T(8,128)S(1)}, f32[2,512,128]{2,1,0:T(8,128)}, u32[]{:S(2)}) copy-start(f32[2,512,128]{2,1,0:T(8,128)} %get-tuple-element.41) | copy-start | bytes 1572868
  90.8 0.8 copy-start.6
  91.6 0.7 copy-start.5
where the time goes:
time: 93.1 us; the launch traced here: 92.8 us
  Pallas kernels  80.9 us (87%)
  local copies, waits for them, and re-layouts  11.3 us (12%)
    pallas_call x1, Pallas kernels, on_device(): pl.pallas_call(lambda *refs: step_kernel(grad_norm, *refs), name='ocean_s...  80.9 us
    unnamed x32, local copies, waits for them, and re-layouts  9.79 us

commit v1 on v0

--- a/solution.py
+++ b/solution.py
@@ -16,6 +16,9 @@
 INV_ROOT_TWO_PI = 0.3989422804014327
 MESH_ID = pl.DeviceIdType.MESH
 GROUP = 16
+LINE = 8
+PIECE = 32
+PART = PIECE // LINE
 ROWS = 45
 COLS = 24
 MARGIN = 3
@@ -27,18 +30,12 @@
 
 def position():
     lon = lax.axis_index("lon")
-    lat = lax.axis_index("lat")
-    z = lon // 4
-    y_hi = lax.rem(lon // 2, 2)
-    core = lax.rem(lon, 2)
-    plane = y_hi * 8 + lat
-    line = z * 2 + core
-    return plane, line
-
-
-def plane_peer(plane, line):
-    lon = (line // 2) * 4 + (plane // 8) * 2 + lax.rem(line, 2)
-    return {"lon": lon, "lat": lax.rem(plane, 8)}
+    plane = lax.rem(lon // 2, 2) * 8 + lax.axis_index("lat")
+    return plane, lon // 4, lax.rem(lon, 2)
+
+
+def device(plane, z, core):
+    return {"lon": z * 4 + (plane // 8) * 2 + core, "lat": lax.rem(plane, 8)}
 
 
 def beside(east, south):
@@ -49,64 +46,81 @@
 
 
 def greet(barrier):
-    plane, line = position()
-
-    def one(k, carry):
-        other = lax.rem(plane + k, GROUP)
-        pl.semaphore_signal(
-            barrier, inc=1, device_id=plane_peer(other, line), device_id_type=MESH_ID
-        )
-        other = lax.rem(line + k, GROUP)
-        pl.semaphore_signal(
-            barrier, inc=1, device_id=plane_peer(plane, other), device_id_type=MESH_ID
-        )
+    plane, z, core = position()
+
+    def signal(target):
+        pl.semaphore_signal(barrier, inc=1, device_id=target, device_id_type=MESH_ID)
+
+    for east, south in AROUND:
+        signal(beside(east, south))
+    signal(device(plane, z, 1 - core))
+
+    def in_plane(k, carry):
+        signal(device(lax.rem(plane + k, GROUP), z, core))
         return carry
 
-    lax.fori_loop(1, GROUP, one, 0)
-    for east, south in AROUND:
-        pl.semaphore_signal(
-            barrier, inc=1, device_id=beside(east, south), device_id_type=MESH_ID
-        )
-    pl.semaphore_wait(barrier, 2 * (GROUP - 1) + len(AROUND))
+    def in_line(k, carry):
+        signal(device(plane, lax.rem(z + k, LINE), core))
+        return carry
+
+    lax.fori_loop(1, GROUP, in_plane, 0)
+    lax.fori_loop(1, LINE, in_line, 0)
+    pl.semaphore_wait(barrier, GROUP + LINE - 1 + len(AROUND))
 
 
 class Exchange:
-    def __init__(self, kind, scatter, src, dst, send, recv):
-        self.plane, self.line = position()
-        self.kind = kind
-        self.scatter = scatter
-        self.src, self.dst, self.send, self.recv = src, dst, send, recv
-        self.me = self.plane if kind == "plane" else self.line
-
-    def copy(self, k):
-        other = lax.rem(self.me + k, GROUP)
+    def __init__(self, kind, scatter, src, dst, sems):
+        self.plane, self.z, self.core = position()
+        self.kind, self.scatter = kind, scatter
+        self.src, self.dst, self.sems = src, dst, sems
+        self.me, self.size = (self.plane, GROUP) if kind == "plane" else (self.z, LINE)
+
+    def copy(self, k, arriving):
+        other = lax.rem(self.me + k, self.size)
         if self.kind == "plane":
-            target = plane_peer(other, self.line)
+            target = device(other, self.z, self.core)
         else:
-            target = plane_peer(self.plane, other)
-        src = self.src.at[other] if self.scatter else self.src
+            target = device(self.plane, other, self.core)
+        if self.scatter:
+            src, slot = self.src.at[other], k
+        else:
+            src = self.src
+            slot = lax.rem(self.me - k + self.size, self.size) if arriving else self.me
         return pltpu.make_async_remote_copy(
             src_ref=src,
-            dst_ref=self.dst.at[k],
-            send_sem=self.send.at[k],
-            recv_sem=self.recv.at[k],
+            dst_ref=self.dst.at[slot],
+            send_sem=self.sems.at[0, k],
+            recv_sem=self.sems.at[1, k],
             device_id=target,
             device_id_type=MESH_ID,
         )
 
     def start(self):
         def one(k, carry):
-            self.copy(k).start()
+            self.copy(k, False).start()
             return carry
 
-        lax.fori_loop(1, GROUP, one, 0)
+        lax.fori_loop(1, self.size, one, 0)
+        return self
 
     def wait(self):
         def one(k, carry):
-            self.copy(k).wait()
+            self.copy(k, True).wait()
             return carry
 
-        lax.fori_loop(1, GROUP, one, 0)
+        lax.fori_loop(1, self.size, one, 0)
+
+
+def to_sibling(src, dst, sems):
+    plane, z, core = position()
+    return pltpu.make_async_remote_copy(
+        src_ref=src,
+        dst_ref=dst,
+        send_sem=sems.at[0],
+        recv_sem=sems.at[1],
+        device_id=device(plane, z, 1 - core),
+        device_id_type=MESH_ID,
+    )
 
 
 def slot_sum(own, slots, count=GROUP):
@@ -215,7 +229,6 @@
 
 
 def step_kernel(
-    grad_norm,
     state,
     land_sea,
     cotangent,
@@ -230,15 +243,7 @@
     layer_scale,
     out,
     grad_state,
-    g_kernel,
-    g_conv,
-    g_gain,
-    g_shift,
-    g_win,
-    g_bias_in,
-    g_wout,
-    g_bias_out,
-    g_scale,
+    gathered,
     win1,
     win2,
     gwin1,
@@ -268,23 +273,27 @@
     h_from_south,
     sem_h,
     small,
+    halves,
+    from_core,
     send_a,
     recv_a,
-    send_b,
-    recv_b,
-    own_b,
-    back_b,
-    own_a,
-    back_a,
-    srecv_a,
-    sown_b,
-    srecv_b,
-    sown_a,
-    sback_a,
-    sem_w,
-    sem_s,
+    tiny_a,
+    line_send,
+    line_recv,
+    line_own,
+    line_all,
+    piece,
+    total,
+    both_halves,
+    seeds,
+    pulled,
+    sem_core,
+    sem_a,
+    sem_tiny,
+    sem_line,
+    sem_back,
 ):
-    plane, line = position()
+    plane, z, core = position()
     greet(pltpu.get_barrier_semaphore())
     halo_bufs = (
         h_east, h_west, h_north, h_south, h_from_west, h_from_east, h_from_north, h_from_south
@@ -299,22 +308,10 @@
     halo = Halo(halo_bufs, sem_h, 0, win1)
     halo.start()
 
-    for blk in range(BLOCKS):
-        for a in range(KSIZE):
-            taps[blk, a, 0:KSIZE, :] = f32(dw_kernel[blk, a])
-    eye = lax.broadcasted_iota(jnp.int32, (COLS, COLS), 0) == lax.broadcasted_iota(
-        jnp.int32, (COLS, COLS), 1
-    )
-    ones = jnp.ones((COLS, C), jnp.float32)
-
-    def spread(i, carry):
-        row = jnp.broadcast_to(land_sea[pl.ds(i, 1), :].astype(jnp.float32), (COLS, COLS))
-        mask[i] = jnp.dot(
-            jnp.where(eye, row, 0.0), ones, preferred_element_type=jnp.float32
-        )
-        return carry
-
-    lax.fori_loop(0, ROWS, spread, 0)
+    taps[...] = f32(dw_kernel[...])
+    ocean_t = land_sea[...].astype(jnp.float32)
+    for i in range(ROWS):
+        mask[i] = jnp.broadcast_to(ocean_t[:, i : i + 1], (COLS, C))
     acc_win[...] = jnp.zeros_like(acc_win)
     acc_wout[...] = jnp.zeros_like(acc_wout)
     acc_rows[...] = jnp.zeros_like(acc_rows)
@@ -324,7 +321,7 @@
     def mix(window, blk):
         start = jnp.broadcast_to(conv_bias[blk : blk + 1, :], (COLS, C))
         rows = convolve(
-            window, lambda a, b: taps[blk, a, b : b + 1, :], lambda base: [start] * 3, False
+            window, lambda a, b: taps[a, b, blk : blk + 1, :], lambda base: [start] * 3, False
         )
 
         def three(g, carry):
@@ -365,25 +362,29 @@
         ocean = mask[pl.ds(c * STRIP, STRIP)].reshape(CELLS, C)
         return (inner + layer_scale[blk : blk + 1, :] * branch_c) * ocean
 
-    def backward(c, incoming, gwindow, blk, keep):
+    def seed(c, incoming, blk):
         ocean = mask[pl.ds(c * STRIP, STRIP)].reshape(CELLS, C)
         masked = incoming * ocean
         upstream[pl.ds(c * STRIP, STRIP)] = masked.reshape(STRIP, COLS, C)
         gb = bf16(masked * layer_scale[blk : blk + 1, :])
+        acc_rows[blk, 3] += fold(f32(gb))
+        seeds[c] = gb
+        pulled[c] = lax.dot_general(
+            gb, weight_out[blk], (((1,), (1,)), ((), ())), preferred_element_type=jnp.float32
+        )
+
+    def backward(c, gwindow, blk, keep):
+        masked = upstream[pl.ds(c * STRIP, STRIP)].reshape(CELLS, C)
         acc_rows[blk, 4] += fold(masked * branch[keep])
-        acc_rows[blk, 3] += fold(f32(gb))
         rows_rows = (((0,), (0,)), ((), ()))
         cols_cols = (((1,), (1,)), ((), ()))
         acc_wout[blk] += lax.dot_general(
-            gb, bf16(active[keep]), rows_rows, preferred_element_type=jnp.float32
-        )
-        hidden[...] = lax.dot_general(
-            gb, weight_out[blk], cols_cols, preferred_element_type=jnp.float32
+            seeds[c], bf16(active[keep]), rows_rows, preferred_element_type=jnp.float32
         )
 
         def through(t, total):
             rows = pl.ds(pl.multiple_of(t * COLS, 8), COLS)
-            gh = f32(bf16(hidden[rows, :] * slope[keep, rows, :]))
+            gh = f32(bf16(pulled[c, rows, :] * slope[keep, rows, :]))
             hidden[rows, :] = gh
             return total + fold(gh)
 
@@ -404,7 +405,7 @@
         acc_rows[blk, 0] += fold(gm)
         gwindow[pl.ds(MARGIN + c * STRIP, STRIP), middle, :] = gm.reshape(STRIP, COLS, C)
 
-    def tap_sums(window, gwindow, blk):
+    def tap_sums(window, gwindow, blk, begin, end):
         def three(g, carry):
             base = g * 3
             grads = [gwindow[base + MARGIN + o, middle, :] for o in range(3)]
@@ -421,12 +422,12 @@
                     acc_taps[blk, a * KSIZE + b] += fold(parts[a])
             return carry
 
-        lax.fori_loop(0, ROWS // 3, three, 0)
-
-    def adjoint(gwindow, blk, put):
+        lax.fori_loop(begin, end, three, 0)
+
+    def adjoint(gwindow, blk, put, begin, end):
         rows = convolve(
             gwindow,
-            lambda a, b: taps[blk, a, b : b + 1, :],
+            lambda a, b: taps[a, b, blk : blk + 1, :],
             lambda base: [upstream[base + o] for o in range(3)],
             True,
         )
@@ -437,66 +438,26 @@
                 put(g * 3 + o, sums[o])
             return carry
 
-        lax.fori_loop(0, ROWS // 3, three, 0)
-
-    def scatter_weights(blk):
+        lax.fori_loop(begin, end, three, 0)
+
+    def core_sum(blk):
         for q in range(4):
-            for half in range(2):
-                send_a[blk, 2 * q + half] = bf16(
-                    acc_win[blk, half * 64 : half * 64 + 64, q * 128 : q * 128 + 128]
-                )
-            turned = jnp.transpose(acc_wout[blk, :, q * 128 : q * 128 + 128])
-            for half in range(2):
-                send_a[blk, 8 + 2 * q + half] = bf16(turned[half * 64 : half * 64 + 64])
-        ex = Exchange(
-            "plane", True, send_a.at[blk], recv_a.at[blk], sem_w.at[blk, 0], sem_w.at[blk, 1]
-        )
-        ex.start()
-        return ex
-
-    def line_scatter(ex, blk):
+            block = slice(q * 128, q * 128 + 128)
+            halves[blk, 0, block, :] = bf16(acc_win[blk, :, block])
+            halves[blk, 1, block, :] = bf16(jnp.transpose(acc_wout[blk, :, block]))
+        copy = to_sibling(halves.at[blk, 1 - core], from_core.at[blk], sem_core.at[blk])
+        copy.start()
+        return copy
+
+    def plane_sum(copy, blk):
+        copy.wait()
+        both = f32(halves[blk, core]) + f32(from_core[blk])
+        send_a[blk] = bf16(both).reshape(GROUP, PIECE, C)
+        return Exchange("plane", True, send_a.at[blk], recv_a.at[blk], sem_a.at[blk]).start()
+
+    def add_slots(ex, blk):
         ex.wait()
-        total = slot_sum(f32(send_a[blk, plane]), recv_a.at[blk])
-        for j in range(GROUP):
-            send_b[blk, j] = total[j * 4 : j * 4 + 4]
-        ex = Exchange(
-            "line", True, send_b.at[blk], recv_b.at[blk], sem_w.at[blk, 2], sem_w.at[blk, 3]
-        )
-        ex.start()
-        return ex
-
-    def line_gather(ex, blk):
-        ex.wait()
-        own_b[blk] = slot_sum(send_b[blk, line], recv_b.at[blk])
-        ex = Exchange(
-            "line", False, own_b.at[blk], back_b.at[blk], sem_w.at[blk, 4], sem_w.at[blk, 5]
-        )
-        ex.start()
-        return ex
-
-    def plane_gather(ex, blk):
-        ex.wait()
-        back_b[blk, 0] = own_b[blk]
-        for j in range(GROUP):
-            sub = back_b[blk, lax.rem(line - j + GROUP, GROUP)]
-            own_a[blk, j * 4 : j * 4 + 4] = bf16(sub)
-        ex = Exchange(
-            "plane", False, own_a.at[blk], back_a.at[blk], sem_w.at[blk, 6], sem_w.at[blk, 7]
-        )
-        ex.start()
-        return ex
-
-    def finish_weights(ex, blk):
-        ex.wait()
-        back_a[blk, 0] = own_a[blk]
-        for p in range(GROUP):
-            piece = f32(back_a[blk, lax.rem(plane - p + GROUP, GROUP)]) * grad_norm
-            if p < 8:
-                g_win[
-                    blk, (p % 2) * 64 : (p % 2) * 64 + 64, (p // 2) * 128 : (p // 2) * 128 + 128
-                ] = piece
-            else:
-                g_wout[blk, (p - 8) * 64 : (p - 8) * 64 + 64] = piece
+        total[blk] = slot_sum(f32(send_a[blk, plane]), recv_a.at[blk])
 
     def small_row(blk, r, value):
         i = blk * 4 + r % 4
@@ -524,68 +485,121 @@
     halo = Halo(halo_bufs, sem_h, 1, win2)
     halo.start()
     small[...] = jnp.zeros_like(small)
+
+    def seed_two(c, carry):
+        seed(c, f32(cotangent[pl.ds(c * STRIP, STRIP)]).reshape(CELLS, C), 1)
+        return carry
+
+    lax.fori_loop(0, CHUNKS, seed_two, 0)
     halo.finish()
     mix(win2, 1)
 
     def both(c, carry):
         result = forward(c, win2, 1, CHUNKS)
         out[pl.ds(c * STRIP, STRIP)] = bf16(result.reshape(STRIP, COLS, C))
-        incoming = f32(cotangent[pl.ds(c * STRIP, STRIP)]).reshape(CELLS, C)
-        backward(c, incoming, gwin2, 1, CHUNKS)
+        backward(c, gwin2, 1, CHUNKS)
         return carry
 
     lax.fori_loop(0, CHUNKS, both, 0)
     halo = Halo(halo_bufs, sem_h, 2, gwin2)
     halo.start()
-    second = scatter_weights(1)
-    tap_sums(win2, gwin2, 1)
+    second = core_sum(1)
+    tap_sums(win2, gwin2, 1, 0, 15)
+    second = plane_sum(second, 1)
     halo.finish()
 
     def put_mixed(row, value):
         mixed[row] = f32(bf16(value))
 
-    adjoint(gwin2, 1, put_mixed)
-    second = line_scatter(second, 1)
+    adjoint(gwin2, 1, put_mixed, 0, 15)
 
     def backward_one(c, carry):
-        incoming = mixed[pl.ds(c * STRIP, STRIP)].reshape(CELLS, C)
-        backward(c, incoming, gwin1, 0, c)
+        seed(c, mixed[pl.ds(c * STRIP, STRIP)].reshape(CELLS, C), 0)
+        backward(c, gwin1, 0, c)
         return carry
 
     lax.fori_loop(0, CHUNKS, backward_one, 0)
     halo = Halo(halo_bufs, sem_h, 3, gwin1)
     halo.start()
-    first = scatter_weights(0)
-    second = line_gather(second, 1)
-    tap_sums(win1, gwin1, 0)
+    first = core_sum(0)
     pack_rows(1)
+    tap_sums(win1, gwin1, 0, 0, 6)
+    first = plane_sum(first, 0)
+    tap_sums(win1, gwin1, 0, 6, 15)
     pack_rows(0)
-    tiny = Exchange("plane", True, small, srecv_a, sem_s.at[0], sem_s.at[1])
-    tiny.start()
-    first = line_scatter(first, 0)
+    tiny = Exchange("plane", True, small, tiny_a, sem_tiny).start()
     halo.finish()
 
     def put_state(row, value):
         grad_state[row] = bf16(value)
 
-    adjoint(gwin1, 0, put_state)
-    first = line_gather(first, 0)
+    adjoint(gwin1, 0, put_state, 0, 8)
+    add_slots(second, 1)
+    add_slots(first, 0)
     tiny.wait()
-    sown_b[...] = slot_sum(small[plane], srecv_a)
-    tiny = Exchange("line", False, sown_b, srecv_b, sem_s.at[2], sem_s.at[3])
-    tiny.start()
-    second = plane_gather(second, 1)
-    first = plane_gather(first, 0)
-    tiny.wait()
-    sown_a[...] = slot_sum(sown_b[...], srecv_b)
-    tiny = Exchange("plane", False, sown_a, sback_a, sem_s.at[4], sem_s.at[5])
-    tiny.start()
-    finish_weights(second, 1)
-    finish_weights(first, 0)
-    tiny.wait()
-    sback_a[0] = sown_a[...]
+    tiny_total = slot_sum(small[plane], tiny_a)
+    for j in range(LINE):
+        line_send[j, 0:PART] = total[0, j * PART : j * PART + PART]
+        line_send[j, PART : 2 * PART] = total[1, j * PART : j * PART + PART]
+        line_send[j, 2 * PART : 2 * PART + 1] = tiny_total[j : j + 1]
+    line = Exchange("line", True, line_send, line_recv, sem_line.at[0]).start()
+    adjoint(gwin1, 0, put_state, 8, 15)
+    line.wait()
+    own = slot_sum(line_send[z], line_recv, LINE)
+    line_own[...] = own
+    line = Exchange("line", False, line_own, line_all, sem_line.at[1]).start()
+    line.wait()
+    line_all[z] = own
+    for j in range(LINE):
+        piece[j * PART : j * PART + PART] = line_all[j, 0:PART]
+        piece[PIECE + j * PART : PIECE + j * PART + PART] = line_all[j, PART : 2 * PART]
+        piece[2 * PIECE + j : 2 * PIECE + j + 1] = line_all[j, 2 * PART : 2 * PART + 1]
+    both_halves[core, plane] = bf16(piece[...])
+    back = Exchange(
+        "plane", False, both_halves.at[core, plane], both_halves.at[core], sem_back
+    ).start()
+    back.wait()
+    swap = to_sibling(both_halves.at[core], both_halves.at[core], sem_core.at[BLOCKS])
+    swap.start()
+    swap.wait()
+    gathered[...] = both_halves[...]
+
+
+def write_kernel(
+    grad_norm,
+    out_from,
+    state_from,
+    gathered,
+    out,
+    grad_state,
+    g_kernel,
+    g_conv,
+    g_gain,
+    g_shift,
+    g_win,
+    g_bias_in,
+    g_wout,
+    g_bias_out,
+    g_scale,
+    small,
+    sems,
+):
+    moves = [
+        pltpu.make_async_copy(out_from, out, sems.at[0]),
+        pltpu.make_async_copy(state_from, grad_state, sems.at[1]),
+    ]
+    for move in moves:
+        move.start()
+    for blk in range(BLOCKS):
+        rows = slice(blk * PIECE, blk * PIECE + PIECE)
+        for p in range(GROUP):
+            g_win[
+                blk, (p % 4) * PIECE : (p % 4) * PIECE + PIECE, (p // 4) * 128 : (p // 4) * 128 + 128
+            ] = f32(gathered[0, p, rows, :]) * grad_norm
+            g_wout[blk, p * PIECE : p * PIECE + PIECE] = f32(gathered[1, p, rows, :]) * grad_norm
+    tiny = slice(2 * PIECE, 2 * PIECE + 8)
     for p in range(GROUP):
-        small[p] = sback_a[lax.rem(plane - p + GROUP, GROUP)] * grad_norm
+        small[p] = (f32(gathered[0, p, tiny, :]) + f32(gathered[1, p, tiny, :])) * grad_norm
     for blk in range(BLOCKS):
 
         def row_of(r):
@@ -593,15 +607,24 @@
 
         for a in range(KSIZE):
             for b in range(KSIZE):
-                g_kernel[blk, a, b : b + 1, :] = row_of(a * KSIZE + b)
+                g_kernel[a, b, blk : blk + 1, :] = row_of(a * KSIZE + b)
         for k, ref in enumerate((g_conv, g_gain, g_shift, g_bias_out, g_scale)):
             ref[blk : blk + 1, :] = row_of(49 + k)
         for q in range(4):
             g_bias_in[blk : blk + 1, q * 128 : q * 128 + 128] = row_of(54 + q)
-
-
-def on_device(*arrays):
+    for move in moves:
+        move.wait()
+
+
+def on_device(
+    state,
+    land_sea,
+    cotangent,
+    dw_kernel,
+    *rest,
+):
     vmem = pl.BlockSpec(memory_space=pltpu.VMEM)
+    anywhere = pl.BlockSpec(memory_space=pl.ANY)
     grad_norm = 1.0 / math.sqrt(
         lax.axis_size("lat") * ROWS * lax.axis_size("lon") * COLS
     )
@@ -611,32 +634,28 @@
     def vm(*shape, dtype=jnp.float32):
         return pltpu.VMEM(shape, dtype)
 
+    def sems(*shape):
+        return pltpu.SemaphoreType.DMA(shape)
+
     tall, wide = ROWS + 2 * MARGIN, COLS + 8
     half = jnp.bfloat16
-    return pl.pallas_call(
-        lambda *refs: step_kernel(grad_norm, *refs),
+    packed = 2 * PIECE + 8
+    fields = pl.pallas_call(
+        step_kernel,
         name="ocean_step",
         out_shape=(
             field,
             field,
-            jax.ShapeDtypeStruct((BLOCKS, KSIZE, KSIZE, C), jnp.float32),
-            row,
-            row,
-            row,
-            jax.ShapeDtypeStruct((BLOCKS, C, F), jnp.float32),
-            jax.ShapeDtypeStruct((BLOCKS, F), jnp.float32),
-            jax.ShapeDtypeStruct((BLOCKS, F, C), jnp.float32),
-            row,
-            row,
+            jax.ShapeDtypeStruct((2, GROUP, packed, C), jnp.bfloat16),
         ),
         in_specs=[vmem] * 12,
-        out_specs=(vmem,) * 11,
+        out_specs=(vmem,) * 3,
         scratch_shapes=[
             vm(tall, wide, C),
             vm(tall, wide, C),
             vm(tall, wide, C),
             vm(tall, wide, C),
-            vm(BLOCKS, KSIZE, 8, C),
+            vm(KSIZE, KSIZE, BLOCKS, C),
             vm(ROWS, COLS, C),
             vm(ROWS, COLS, C),
             vm(CELLS, F),
@@ -659,28 +678,54 @@
             vm(4, tall, MARGIN, C, dtype=half),
             vm(4, MARGIN, COLS, C, dtype=half),
             vm(4, MARGIN, COLS, C, dtype=half),
-            pltpu.SemaphoreType.DMA((4, 2, len(AROUND))),
+            sems(4, 2, len(AROUND)),
             vm(GROUP, 8, C),
-            vm(BLOCKS, GROUP, 64, C, dtype=half),
-            vm(BLOCKS, GROUP, 64, C, dtype=half),
-            vm(BLOCKS, GROUP, 4, C),
-            vm(BLOCKS, GROUP, 4, C),
-            vm(BLOCKS, 4, C),
-            vm(BLOCKS, GROUP, 4, C),
-            vm(BLOCKS, 64, C, dtype=half),
-            vm(BLOCKS, GROUP, 64, C, dtype=half),
+            vm(BLOCKS, 2, F, C, dtype=half),
+            vm(BLOCKS, F, C, dtype=half),
+            vm(BLOCKS, GROUP, PIECE, C, dtype=half),
+            vm(BLOCKS, GROUP, PIECE, C, dtype=half),
             vm(GROUP, 8, C),
-            vm(8, C),
-            vm(GROUP, 8, C),
-            vm(8, C),
-            vm(GROUP, 8, C),
-            pltpu.SemaphoreType.DMA((BLOCKS, 8, GROUP)),
-            pltpu.SemaphoreType.DMA((6, GROUP)),
+            vm(LINE, 2 * PART + 1, C),
+            vm(LINE, 2 * PART + 1, C),
+            vm(2 * PART + 1, C),
+            vm(LINE, 2 * PART + 1, C),
+            vm(packed, C),
+            vm(BLOCKS, PIECE, C),
+            vm(2, GROUP, packed, C, dtype=half),
+            vm(CHUNKS, CELLS, C, dtype=half),
+            vm(CHUNKS, CELLS, F),
+            sems(BLOCKS + 1, 2),
+            sems(BLOCKS, 2, GROUP),
+            sems(2, GROUP),
+            sems(2, 2, LINE),
+            sems(2, GROUP),
         ],
         compiler_params=pltpu.CompilerParams(
-            collective_id=0, has_side_effects=True, vmem_limit_bytes=56 << 20
+            collective_id=0, has_side_effects=True, vmem_limit_bytes=40 << 20
         ),
-    )(*arrays)
+    )(state, land_sea.T, cotangent, jnp.transpose(dw_kernel, (1, 2, 0, 3)), *rest)
+    results = pl.pallas_call(
+        lambda *refs: write_kernel(grad_norm, *refs),
+        name="write_results",
+        out_shape=(
+            field,
+            field,
+            jax.ShapeDtypeStruct((KSIZE, KSIZE, BLOCKS, C), jnp.float32),
+            row,
+            row,
+            row,
+            jax.ShapeDtypeStruct((BLOCKS, C, F), jnp.float32),
+            jax.ShapeDtypeStruct((BLOCKS, F), jnp.float32),
+            jax.ShapeDtypeStruct((BLOCKS, F, C), jnp.float32),
+            row,
+            row,
+        ),
+        in_specs=[anywhere, anywhere, vmem],
+        out_specs=(anywhere, anywhere) + (vmem,) * 9,
+        scratch_shapes=[vm(GROUP, 8, C), sems(2)],
+        compiler_params=pltpu.CompilerParams(vmem_limit_bytes=16 << 20),
+    )(*fields)
+    return results[:2] + (jnp.transpose(results[2], (2, 0, 1, 3)),) + results[3:]
 
 
 def solution(mesh):

time: 93.1 us -> 85.8 us (0.922)
  Pallas kernels: 80.9 us -> 76.8 us
  local copies, waits for them, and re-layouts: 11.3 us -> 7.98 us
    pallas_call x1 -> x2, Pallas kernels: 80.9 us -> 76.8 us  [the longest x1 74.9 us: on_device(): pl.pallas_call(step_kernel, name='ocean_step', out_shape=(field, field, j...]
    unnamed x32 -> x24, local copies, waits for them, and re-layouts: 9.79 us -> 7.98 us
    pallas_call x1 -> x0, local copies, waits for them, and re-layouts: 1.51 us -> none  [on_device(): pl.pallas_call(lambda *refs: step_kernel(grad_norm, *refs), name='ocean_s...]
where the time goes in v1:
time: 85.8 us; the launch traced here: 85.4 us
  Pallas kernels  76.8 us (90%)
  local copies, waits for them, and re-layouts  7.98 us (9%)
    pallas_call x1, Pallas kernels, on_device(): pl.pallas_call(step_kernel, name='ocean_step', out_shape=(field, field, j...  74.9 us
    unnamed x24, local copies, waits for them, and re-layouts  7.98 us
    pallas_call x1, Pallas kernels, on_device(): pl.pallas_call(lambda *refs: write_kernel(grad_norm, *refs), name='write_...  1.82 us

profile of v1, /device:TPU:1, one launch (start us, length us, event | category | flops | bytes accessed | tf_op | source)
XLA Modules:
  0.0 85.4 jit_solution(6958037051568745051)
XLA Ops:
  0.6 0.0 copy-start.8
  0.7 0.0 copy-start.9
  0.7 0.0 copy-start.7
  0.7 0.7 copy-done.8
  1.3 0.0 copy-done.9
  1.3 0.0 copy-done.7
  1.4 0.0 copy-start
  1.4 1.0 %copy-done = bf16[45,24,128]{2,1,0:T(8,128)(2,1)S(1)} copy-done((bf16[45,24,128]{2,1,0:T(8,128)(2,1)S(1)}, bf16[45,24,128]{2,1,0:T(8,128)(2,1)}, u32[]{:S(2)}) %copy-start) | copy-done | bytes 276504
  2.3 1.0 %copy-done.1 = bf16[45,24,128]{2,1,0:T(8,128)(2,1)S(1)} copy-done((bf16[45,24,128]{2,1,0:T(8,128)(2,1)S(1)}, bf16[45,24,128]{2,1,0:T(8,128)(2,1)}, u32[]{:S(2)}) %copy-start.1) | copy-done | bytes 276504
  3.3 0.0 copy-start.2
  3.3 0.9 %copy-done.2 = bf16[2,128,512]{2,1,0:T(8,128)(2,1)S(1)} copy-done((bf16[2,128,512]{2,1,0:T(8,128)(2,1)S(1)}, bf16[2,128,512]{2,1,0:T(8,128)(2,1)}, u32[]{:S(2)}) %copy-start.2) | copy-done | bytes 262168
  4.2 0.0 copy-start.3
  4.2 0.9 %copy-done.3 = bf16[2,512,128]{2,1,0:T(8,128)(2,1)S(1)} copy-done((bf16[2,512,128]{2,1,0:T(8,128)(2,1)S(1)}, bf16[2,512,128]{2,1,0:T(8,128)(2,1)}, u32[]{:S(2)}) %copy-start.3) | copy-done | bytes 262168
  5.2 0.0 copy-start.4
  5.2 0.7 copy-done.4
  5.9 0.0 copy-start.5
  5.9 0.7 copy-done.5
  6.6 0.0 copy-start.6
  6.6 0.7 copy-done.6
  7.3 0.0 copy-start.10
  7.3 0.7 copy-done.10
  8.0 0.7 copy-done.11
  8.7 74.9 %ocean_step.1 = (bf16[45,24,128]{2,1,0:T(8,128)(2,1)S(1)}, bf16[45,24,128]{2,1,0:T(8,128)(2,1)S(1)}, bf16[2,16,72,128]{3,2,1,0:T(8,128)(2,1)S(1)}) custom-call(bf16[45,24,128]{2,1,0:T(8,128)(2,1)S(1)} %copy-done, s32[24,45]{1,0:T(8,128)S(1)} %bitcast.4, bf16[45,24,128]{2,1,0:T(8,128)(2,1)S(1)} %copy-done.1, bf16[7,7,2,128]{3,2,1,0:T(2,128)(2,1)S(1)} %bitcast.3, ...), custom_call_target="tpu_custom_call" | custom-call | tf_op jit(solution)/shard_map/ocean_step/pallas_call | solution.py:643
  83.6 1.8 %write_results.1 = (bf16[45,24,128]{2,1,0:T(8,128)(2,1)}, bf16[45,24,128]{2,1,0:T(8,128)(2,1)}, f32[7,7,2,128]{3,2,1,0:T(2,128)}, f32[2,128]{1,0:T(2,128)}, f32[...) custom-call(bf16[45,24,128]{2,1,0:T(8,128)(2,1)S(1)} %get-tuple-elem, ...), custom_call_target="tpu_custom_call" | custom-call | tf_op jit(solution)/shard_map/write_results/pallas_call | solution.py:707
  (2 shorter events, 0.0 us)
Async XLA Ops:
  0.6 0.7 copy-start.8
  0.7 0.7 copy-start.9
  0.7 0.7 copy-start.7
  1.4 1.0 %copy-start = (bf16[45,24,128]{2,1,0:T(8,128)(2,1)S(1)}, bf16[45,24,128]{2,1,0:T(8,128)(2,1)}, u32[]{:S(2)}) copy-start(bf16[45,24,128]{2,1,0:T(8,128)(2,1)} %state.1) | copy-start | bytes 829444
  2.3 1.0 %copy-start.1 = (bf16[45,24,128]{2,1,0:T(8,128)(2,1)S(1)}, bf16[45,24,128]{2,1,0:T(8,128)(2,1)}, u32[]{:S(2)}) copy-start(bf16[45,24,128]{2,1,0:T(8,128)(2,1)} %cotangent.1) | copy-start | bytes 829444
  3.3 0.9 %copy-start.2 = (bf16[2,128,512]{2,1,0:T(8,128)(2,1)S(1)}, bf16[2,128,512]{2,1,0:T(8,128)(2,1)}, u32[]{:S(2)}) copy-start(bf16[2,128,512]{2,1,0:T(8,128)(2,1)} %weight_in.1) | copy-start | bytes 786436
  4.2 0.9 %copy-start.3 = (bf16[2,512,128]{2,1,0:T(8,128)(2,1)S(1)}, bf16[2,512,128]{2,1,0:T(8,128)(2,1)}, u32[]{:S(2)}) copy-start(bf16[2,512,128]{2,1,0:T(8,128)(2,1)} %weight_out.1) | copy-start | bytes 786436
  5.2 0.7 copy-start.4
  5.9 0.7 copy-start.5
  6.6 0.7 copy-start.6
  7.3 0.7 copy-start.10
  8.0 0.7 copy-start.11

commit v2 on v1

--- a/solution.py
+++ b/solution.py
@@ -172,6 +172,10 @@
         ]
 
     def start(self):
+        self.stage()
+        self.launch()
+
+    def stage(self):
         east, west, north, south = self.bufs[:4]
         window = self.window
         inner = slice(MARGIN, MARGIN + ROWS)
@@ -179,6 +183,8 @@
         west[...] = bf16(window[inner, MARGIN : 2 * MARGIN, :])
         north[...] = bf16(window[MARGIN : 2 * MARGIN, MARGIN : MARGIN + COLS, :])
         south[...] = bf16(window[ROWS : ROWS + MARGIN, MARGIN : MARGIN + COLS, :])
+
+    def launch(self):
         for copy in self.copies:
             copy.start()
 
@@ -229,20 +235,12 @@
 
 
 def step_kernel(
-    state,
-    land_sea,
-    cotangent,
-    dw_kernel,
-    conv_bias,
-    norm_gain,
-    norm_bias,
-    weight_in,
-    bias_in,
-    weight_out,
-    bias_out,
-    layer_scale,
-    out,
-    grad_state,
+    *refs,
+):
+    arguments, refs = refs[:12], refs[12:]
+    (
+    out_hbm,
+    state_hbm,
     gathered,
     win1,
     win2,
@@ -292,9 +290,34 @@
     sem_tiny,
     sem_line,
     sem_back,
-):
+    sem_load,
+    out,
+    grad_state,
+    sem_put,
+    *arrived,
+    ) = refs
+    loads = [
+        pltpu.make_async_copy(source, target, sem_load.at[n])
+        for n, (source, target) in enumerate(zip(arguments, arrived))
+    ]
+    for load in loads:
+        load.start()
+    (
+        state,
+        land_sea,
+        cotangent,
+        dw_kernel,
+        conv_bias,
+        norm_gain,
+        norm_bias,
+        weight_in,
+        bias_in,
+        weight_out,
+        bias_out,
+        layer_scale,
+    ) = arrived
     plane, z, core = position()
-    greet(pltpu.get_barrier_semaphore())
+    loads[0].wait()
     halo_bufs = (
         h_east, h_west, h_north, h_south, h_from_west, h_from_east, h_from_north, h_from_south
     )
@@ -306,7 +329,11 @@
 
     lax.fori_loop(0, CHUNKS, widen, 0)
     halo = Halo(halo_bufs, sem_h, 0, win1)
-    halo.start()
+    halo.stage()
+    greet(pltpu.get_barrier_semaphore())
+    halo.launch()
+    for load in loads[1:]:
+        load.wait()
 
     taps[...] = f32(dw_kernel[...])
     ocean_t = land_sea[...].astype(jnp.float32)
@@ -501,6 +528,8 @@
         return carry
 
     lax.fori_loop(0, CHUNKS, both, 0)
+    put_out = pltpu.make_async_copy(out, out_hbm, sem_put.at[0])
+    put_out.start()
     halo = Halo(halo_bufs, sem_h, 2, gwin2)
     halo.start()
     second = core_sum(1)
@@ -544,6 +573,8 @@
         line_send[j, 2 * PART : 2 * PART + 1] = tiny_total[j : j + 1]
     line = Exchange("line", True, line_send, line_recv, sem_line.at[0]).start()
     adjoint(gwin1, 0, put_state, 8, 15)
+    put_grad = pltpu.make_async_copy(grad_state, state_hbm, sem_put.at[1])
+    put_grad.start()
     line.wait()
     own = slot_sum(line_send[z], line_recv, LINE)
     line_own[...] = own
@@ -562,7 +593,11 @@
     swap = to_sibling(both_halves.at[core], both_halves.at[core], sem_core.at[BLOCKS])
     swap.start()
     swap.wait()
-    gathered[...] = both_halves[...]
+    put_sums = pltpu.make_async_copy(both_halves, gathered, sem_put.at[2])
+    put_sums.start()
+    put_out.wait()
+    put_grad.wait()
+    put_sums.wait()
 
 
 def write_kernel(
@@ -582,14 +617,19 @@
     g_bias_out,
     g_scale,
     small,
+    held,
     sems,
 ):
+    pairs = ((out_from, out), (state_from, grad_state))
     moves = [
-        pltpu.make_async_copy(out_from, out, sems.at[0]),
-        pltpu.make_async_copy(state_from, grad_state, sems.at[1]),
+        pltpu.make_async_copy(pair[0], held.at[n], sems.at[n]) for n, pair in enumerate(pairs)
     ]
     for move in moves:
         move.start()
+    for n, pair in enumerate(pairs):
+        moves[n].wait()
+        moves[n] = pltpu.make_async_copy(held.at[n], pair[1], sems.at[2 + n])
+        moves[n].start()
     for blk in range(BLOCKS):
         rows = slice(blk * PIECE, blk * PIECE + PIECE)
         for p in range(GROUP):
@@ -640,6 +680,7 @@
     tall, wide = ROWS + 2 * MARGIN, COLS + 8
     half = jnp.bfloat16
     packed = 2 * PIECE + 8
+    arguments = (state, land_sea.T, cotangent, jnp.transpose(dw_kernel, (1, 2, 0, 3)), *rest)
     fields = pl.pallas_call(
         step_kernel,
         name="ocean_step",
@@ -648,8 +689,8 @@
             field,
             jax.ShapeDtypeStruct((2, GROUP, packed, C), jnp.bfloat16),
         ),
-        in_specs=[vmem] * 12,
-        out_specs=(vmem,) * 3,
+        in_specs=[pl.BlockSpec(memory_space=pltpu.HBM)] * 12,
+        out_specs=(anywhere,) * 3,
         scratch_shapes=[
             vm(tall, wide, C),
             vm(tall, wide, C),
@@ -699,11 +740,16 @@
             sems(2, GROUP),
             sems(2, 2, LINE),
             sems(2, GROUP),
+            sems(len(arguments)),
+            vm(ROWS, COLS, C, dtype=half),
+            vm(ROWS, COLS, C, dtype=half),
+            sems(3),
+            *(pltpu.VMEM(array.shape, array.dtype) for array in arguments),
         ],
         compiler_params=pltpu.CompilerParams(
-            collective_id=0, has_side_effects=True, vmem_limit_bytes=40 << 20
+            collective_id=0, has_side_effects=True, vmem_limit_bytes=58 << 20
         ),
-    )(state, land_sea.T, cotangent, jnp.transpose(dw_kernel, (1, 2, 0, 3)), *rest)
+    )(*arguments)
     results = pl.pallas_call(
         lambda *refs: write_kernel(grad_norm, *refs),
         name="write_results",
@@ -722,8 +768,12 @@
         ),
         in_specs=[anywhere, anywhere, vmem],
         out_specs=(anywhere, anywhere) + (vmem,) * 9,
-        scratch_shapes=[vm(GROUP, 8, C), sems(2)],
-        compiler_params=pltpu.CompilerParams(vmem_limit_bytes=16 << 20),
+        scratch_shapes=[
+            vm(GROUP, 8, C),
+            vm(2, ROWS, COLS, C, dtype=half),
+            sems(4),
+        ],
+        compiler_params=pltpu.CompilerParams(vmem_limit_bytes=58 << 20),
     )(*fields)
     return results[:2] + (jnp.transpose(results[2], (2, 0, 1, 3)),) + results[3:]
 

time: 85.8 us -> 81.6 us (0.951)
  local copies, waits for them, and re-layouts: 7.98 us -> 0 us
  Pallas kernels: 76.8 us -> 80.7 us
    unnamed x24 -> x0, local copies, waits for them, and re-layouts: 7.98 us -> none
    pallas_call x1, Pallas kernels: 1.82 us -> 3.86 us  [on_device(): pl.pallas_call(lambda *refs: write_kernel(grad_norm, *refs), name='write_...]
    pallas_call x1, Pallas kernels: 74.9 us -> 76.9 us  [on_device(): pl.pallas_call(step_kernel, name='ocean_step', out_shape=(field, field, j...]
where the time goes in v2:
time: 81.6 us; the launch traced here: 81.4 us
  Pallas kernels  80.7 us (99%)
    pallas_call x1, Pallas kernels, on_device(): pl.pallas_call(step_kernel, name='ocean_step', out_shape=(field, field, j...  76.9 us
    pallas_call x1, Pallas kernels, on_device(): pl.pallas_call(lambda *refs: write_kernel(grad_norm, *refs), name='write_...  3.86 us

profile of v2, /device:TPU:1, one launch (start us, length us, event | category | flops | bytes accessed | tf_op | source)
XLA Modules:
  0.0 81.4 jit_solution(1638642231132007976)
XLA Ops:
  0.6 76.9 %ocean_step.1 = (bf16[45,24,128]{2,1,0:T(8,128)(2,1)}, bf16[45,24,128]{2,1,0:T(8,128)(2,1)}, bf16[2,16,72,128]{3,2,1,0:T(8,128)(2,1)}) custom-call(bf16[45,24,128]{2,1,0:T(8,128)(2,1)} %refs_0_.1, s32[24,45]{1,0:T(8,128)} %bitcast.4, bf16[45,24,128]{2,1,0:T(8,128)(2,1)} %refs_2_.1, bf16[7,7,2,128]{3,2,1,0:T(2,128)(2,1)} %bitcast.3, f32[2,128]{1,0:T(2,128)} %refs_4_.1, ...), custom_call_target="tpu_custom_call" | custom-call | tf_op jit(solution)/shard_map/ocean_step/pallas_call | solution.py:684
  77.5 3.9 %write_results.1 = (bf16[45,24,128]{2,1,0:T(8,128)(2,1)}, bf16[45,24,128]{2,1,0:T(8,128)(2,1)}, f32[7,7,2,128]{3,2,1,0:T(2,128)}, f32[2,128]{1,0:T(2,128)}, f32[...) custom-call(bf16[45,24,128]{2,1,0:T(8,128)(2,1)} %get-tuple-element., ...), custom_call_target="tpu_custom_call" | custom-call | tf_op jit(solution)/shard_map/write_results/pallas_call | solution.py:753

commit v3 on v2

--- a/solution.py
+++ b/solution.py
@@ -18,7 +18,6 @@
 GROUP = 16
 LINE = 8
 PIECE = 32
-PART = PIECE // LINE
 ROWS = 45
 COLS = 24
 MARGIN = 3
@@ -45,7 +44,7 @@
     }
 
 
-def greet(barrier):
+def announce(barrier):
     plane, z, core = position()
 
     def signal(target):
@@ -65,7 +64,6 @@
 
     lax.fori_loop(1, GROUP, in_plane, 0)
     lax.fori_loop(1, LINE, in_line, 0)
-    pl.semaphore_wait(barrier, GROUP + LINE - 1 + len(AROUND))
 
 
 class Exchange:
@@ -174,6 +172,13 @@
     def start(self):
         self.stage()
         self.launch()
+
+    def stage_from(self, tile):
+        east, west, north, south = self.bufs[:4]
+        east[...] = tile[:, COLS - MARGIN : COLS, :]
+        west[...] = tile[:, 0:MARGIN, :]
+        north[...] = tile[0:MARGIN]
+        south[...] = tile[ROWS - MARGIN : ROWS]
 
     def stage(self):
         east, west, north, south = self.bufs[:4]
@@ -241,7 +246,8 @@
     (
     out_hbm,
     state_hbm,
-    gathered,
+    sums_one,
+    sums_two,
     win1,
     win2,
     gwin1,
@@ -276,13 +282,10 @@
     send_a,
     recv_a,
     tiny_a,
-    line_send,
-    line_recv,
     line_own,
     line_all,
-    piece,
-    total,
-    both_halves,
+    gather_one,
+    gather_two,
     seeds,
     pulled,
     sem_core,
@@ -317,21 +320,24 @@
         layer_scale,
     ) = arrived
     plane, z, core = position()
+    barrier = pltpu.get_barrier_semaphore()
+    announce(barrier)
     loads[0].wait()
     halo_bufs = (
         h_east, h_west, h_north, h_south, h_from_west, h_from_east, h_from_north, h_from_south
     )
     middle = slice(MARGIN, MARGIN + COLS)
 
+    halo = Halo(halo_bufs, sem_h, 0, win1)
+    halo.stage_from(state)
+    pl.semaphore_wait(barrier, GROUP + LINE - 1 + len(AROUND))
+    halo.launch()
+
     def widen(c, carry):
         win1[pl.ds(MARGIN + c * STRIP, STRIP), middle, :] = f32(state[pl.ds(c * STRIP, STRIP)])
         return carry
 
     lax.fori_loop(0, CHUNKS, widen, 0)
-    halo = Halo(halo_bufs, sem_h, 0, win1)
-    halo.stage()
-    greet(pltpu.get_barrier_semaphore())
-    halo.launch()
     for load in loads[1:]:
         load.wait()
 
@@ -344,6 +350,7 @@
     acc_rows[...] = jnp.zeros_like(acc_rows)
     acc_bias[...] = jnp.zeros_like(acc_bias)
     acc_taps[...] = jnp.zeros_like(acc_taps)
+    small[...] = jnp.zeros_like(small)
 
     def mix(window, blk):
         start = jnp.broadcast_to(conv_bias[blk : blk + 1, :], (COLS, C))
@@ -374,12 +381,12 @@
             h = hidden[rows, :] + bias_in[blk : blk + 1, :]
             cumulative = 0.5 * (1.0 + lax.erf(h * INV_ROOT_TWO))
             density = jnp.exp(-0.5 * h * h) * INV_ROOT_TWO_PI
-            active[keep, rows, :] = h * cumulative
+            active[keep, rows, :] = bf16(h * cumulative)
             slope[keep, rows, :] = cumulative + h * density
             return carry
 
         lax.fori_loop(0, STRIP, gelu, 0)
-        act = bf16(active[keep])
+        act = active[keep]
         branch_c = (
             jnp.dot(act, weight_out[blk], preferred_element_type=jnp.float32)
             + bias_out[blk : blk + 1, :]
@@ -406,17 +413,13 @@
         rows_rows = (((0,), (0,)), ((), ()))
         cols_cols = (((1,), (1,)), ((), ()))
         acc_wout[blk] += lax.dot_general(
-            seeds[c], bf16(active[keep]), rows_rows, preferred_element_type=jnp.float32
-        )
-
-        def through(t, total):
-            rows = pl.ds(pl.multiple_of(t * COLS, 8), COLS)
-            gh = f32(bf16(pulled[c, rows, :] * slope[keep, rows, :]))
-            hidden[rows, :] = gh
-            return total + fold(gh)
-
-        acc_bias[blk] = lax.fori_loop(0, STRIP, through, acc_bias[blk])
-        gh = bf16(hidden[...])
+            seeds[c], active[keep], rows_rows, preferred_element_type=jnp.float32
+        )
+
+        gh = bf16(pulled[c] * slope[keep])
+        acc_bias[blk] += jnp.dot(
+            jnp.ones((8, CELLS), jnp.bfloat16), gh, preferred_element_type=jnp.float32
+        )
         norm = normed[keep]
         gain = norm_gain[blk : blk + 1, :]
         lifted = bf16(norm * gain + norm_bias[blk : blk + 1, :])
@@ -482,9 +485,37 @@
         send_a[blk] = bf16(both).reshape(GROUP, PIECE, C)
         return Exchange("plane", True, send_a.at[blk], recv_a.at[blk], sem_a.at[blk]).start()
 
-    def add_slots(ex, blk):
+    def line_sum(ex, blk, tiny):
         ex.wait()
-        total[blk] = slot_sum(f32(send_a[blk, plane]), recv_a.at[blk])
+        total = bf16(slot_sum(f32(send_a[blk, plane]), recv_a.at[blk]))
+        rows = line_all.at[blk] if tiny is not None else line_all.at[blk, :, 0:PIECE]
+        line_all[blk, z, 0:PIECE] = total
+        line_own[blk, 0:PIECE] = total
+        own = line_own.at[blk, 0:PIECE]
+        if tiny is not None:
+            tiny.wait()
+            tiny_total = bf16(slot_sum(small[plane], tiny_a))
+            line_all[blk, z, PIECE : PIECE + 8] = tiny_total
+            line_own[blk, PIECE : PIECE + 8] = tiny_total
+            own = line_own.at[blk]
+        return Exchange("line", False, own, rows, sem_line.at[blk]).start()
+
+    def plane_back(ex, blk, gather):
+        ex.wait()
+        rows = gather.shape[2]
+        own = f32(line_all[blk, 0, 0:rows])
+        for j in range(1, LINE):
+            own = own + f32(line_all[blk, j, 0:rows])
+        gather[core, plane] = bf16(own)
+        return Exchange(
+            "plane", False, gather.at[core, plane], gather.at[core], sem_back.at[blk]
+        ).start()
+
+    def swap_halves(ex, blk, gather):
+        ex.wait()
+        copy = to_sibling(gather.at[core], gather.at[core], sem_core.at[BLOCKS + blk])
+        copy.start()
+        return copy
 
     def small_row(blk, r, value):
         i = blk * 4 + r % 4
@@ -496,7 +527,7 @@
         for k in range(5):
             small_row(blk, 49 + k, acc_rows[blk, k])
         for q in range(4):
-            small_row(blk, 54 + q, acc_bias[blk, :, q * 128 : q * 128 + 128])
+            small_row(blk, 54 + q, acc_bias[blk, 0:1, q * 128 : q * 128 + 128])
 
     halo.finish()
     mix(win1, 0)
@@ -511,7 +542,6 @@
     lax.fori_loop(0, CHUNKS, forward_one, 0)
     halo = Halo(halo_bufs, sem_h, 1, win2)
     halo.start()
-    small[...] = jnp.zeros_like(small)
 
     def seed_two(c, carry):
         seed(c, f32(cotangent[pl.ds(c * STRIP, STRIP)]).reshape(CELLS, C), 1)
@@ -535,12 +565,14 @@
     second = core_sum(1)
     tap_sums(win2, gwin2, 1, 0, 15)
     second = plane_sum(second, 1)
+    pack_rows(1)
     halo.finish()
 
     def put_mixed(row, value):
         mixed[row] = f32(bf16(value))
 
     adjoint(gwin2, 1, put_mixed, 0, 15)
+    second = line_sum(second, 1, None)
 
     def backward_one(c, carry):
         seed(c, mixed[pl.ds(c * STRIP, STRIP)].reshape(CELLS, C), 0)
@@ -551,60 +583,41 @@
     halo = Halo(halo_bufs, sem_h, 3, gwin1)
     halo.start()
     first = core_sum(0)
-    pack_rows(1)
+    second = plane_back(second, 1, gather_two)
     tap_sums(win1, gwin1, 0, 0, 6)
     first = plane_sum(first, 0)
     tap_sums(win1, gwin1, 0, 6, 15)
     pack_rows(0)
     tiny = Exchange("plane", True, small, tiny_a, sem_tiny).start()
+    second = swap_halves(second, 1, gather_two)
     halo.finish()
 
     def put_state(row, value):
         grad_state[row] = bf16(value)
 
     adjoint(gwin1, 0, put_state, 0, 8)
-    add_slots(second, 1)
-    add_slots(first, 0)
-    tiny.wait()
-    tiny_total = slot_sum(small[plane], tiny_a)
-    for j in range(LINE):
-        line_send[j, 0:PART] = total[0, j * PART : j * PART + PART]
-        line_send[j, PART : 2 * PART] = total[1, j * PART : j * PART + PART]
-        line_send[j, 2 * PART : 2 * PART + 1] = tiny_total[j : j + 1]
-    line = Exchange("line", True, line_send, line_recv, sem_line.at[0]).start()
+    first = line_sum(first, 0, tiny)
     adjoint(gwin1, 0, put_state, 8, 15)
     put_grad = pltpu.make_async_copy(grad_state, state_hbm, sem_put.at[1])
     put_grad.start()
-    line.wait()
-    own = slot_sum(line_send[z], line_recv, LINE)
-    line_own[...] = own
-    line = Exchange("line", False, line_own, line_all, sem_line.at[1]).start()
-    line.wait()
-    line_all[z] = own
-    for j in range(LINE):
-        piece[j * PART : j * PART + PART] = line_all[j, 0:PART]
-        piece[PIECE + j * PART : PIECE + j * PART + PART] = line_all[j, PART : 2 * PART]
-        piece[2 * PIECE + j : 2 * PIECE + j + 1] = line_all[j, 2 * PART : 2 * PART + 1]
-    both_halves[core, plane] = bf16(piece[...])
-    back = Exchange(
-        "plane", False, both_halves.at[core, plane], both_halves.at[core], sem_back
-    ).start()
-    back.wait()
-    swap = to_sibling(both_halves.at[core], both_halves.at[core], sem_core.at[BLOCKS])
-    swap.start()
-    swap.wait()
-    put_sums = pltpu.make_async_copy(both_halves, gathered, sem_put.at[2])
-    put_sums.start()
-    put_out.wait()
-    put_grad.wait()
-    put_sums.wait()
+    second.wait()
+    put_two = pltpu.make_async_copy(gather_two, sums_two, sem_put.at[2])
+    put_two.start()
+    first = plane_back(first, 0, gather_one)
+    first = swap_halves(first, 0, gather_one)
+    first.wait()
+    put_one = pltpu.make_async_copy(gather_one, sums_one, sem_put.at[3])
+    put_one.start()
+    for put in (put_out, put_grad, put_two, put_one):
+        put.wait()
 
 
 def write_kernel(
     grad_norm,
     out_from,
     state_from,
-    gathered,
+    sums_one,
+    sums_two,
     out,
     grad_state,
     g_kernel,
@@ -631,15 +644,16 @@
         moves[n] = pltpu.make_async_copy(held.at[n], pair[1], sems.at[2 + n])
         moves[n].start()
     for blk in range(BLOCKS):
-        rows = slice(blk * PIECE, blk * PIECE + PIECE)
+        sums = (sums_one, sums_two)[blk]
+        rows = slice(0, PIECE)
         for p in range(GROUP):
             g_win[
                 blk, (p % 4) * PIECE : (p % 4) * PIECE + PIECE, (p // 4) * 128 : (p // 4) * 128 + 128
-            ] = f32(gathered[0, p, rows, :]) * grad_norm
-            g_wout[blk, p * PIECE : p * PIECE + PIECE] = f32(gathered[1, p, rows, :]) * grad_norm
-    tiny = slice(2 * PIECE, 2 * PIECE + 8)
+            ] = f32(sums[0, p, rows, :]) * grad_norm
+            g_wout[blk, p * PIECE : p * PIECE + PIECE] = f32(sums[1, p, rows, :]) * grad_norm
+    tiny = slice(PIECE, PIECE + 8)
     for p in range(GROUP):
-        small[p] = (f32(gathered[0, p, tiny, :]) + f32(gathered[1, p, tiny, :])) * grad_norm
+        small[p] = (f32(sums_one[0, p, tiny, :]) + f32(sums_one[1, p, tiny, :])) * grad_norm
     for blk in range(BLOCKS):
 
         def row_of(r):
@@ -679,7 +693,7 @@
 
     tall, wide = ROWS + 2 * MARGIN, COLS + 8
     half = jnp.bfloat16
-    packed = 2 * PIECE + 8
+    packed = PIECE + 8
     arguments = (state, land_sea.T, cotangent, jnp.transpose(dw_kernel, (1, 2, 0, 3)), *rest)
     fields = pl.pallas_call(
         step_kernel,
@@ -688,9 +702,10 @@
             field,
             field,
             jax.ShapeDtypeStruct((2, GROUP, packed, C), jnp.bfloat16),
+            jax.ShapeDtypeStruct((2, GROUP, PIECE, C), jnp.bfloat16),
         ),
         in_specs=[pl.BlockSpec(memory_space=pltpu.HBM)] * 12,
-        out_specs=(anywhere,) * 3,
+        out_specs=(anywhere,) * 4,
         scratch_shapes=[
             vm(tall, wide, C),
             vm(tall, wide, C),
@@ -700,7 +715,7 @@
             vm(ROWS, COLS, C),
             vm(ROWS, COLS, C),
             vm(CELLS, F),
-            vm(CHUNKS + 1, CELLS, F),
+            vm(CHUNKS + 1, CELLS, F, dtype=half),
             vm(CHUNKS + 1, CELLS, F),
             vm(CHUNKS + 1, CELLS, C),
             vm(CHUNKS + 1, CELLS, C),
@@ -726,24 +741,21 @@
             vm(BLOCKS, GROUP, PIECE, C, dtype=half),
             vm(BLOCKS, GROUP, PIECE, C, dtype=half),
             vm(GROUP, 8, C),
-            vm(LINE, 2 * PART + 1, C),
-            vm(LINE, 2 * PART + 1, C),
-            vm(2 * PART + 1, C),
-            vm(LINE, 2 * PART + 1, C),
-            vm(packed, C),
-            vm(BLOCKS, PIECE, C),
+            vm(BLOCKS, packed, C, dtype=half),
+            vm(BLOCKS, LINE, packed, C, dtype=half),
             vm(2, GROUP, packed, C, dtype=half),
+            vm(2, GROUP, PIECE, C, dtype=half),
             vm(CHUNKS, CELLS, C, dtype=half),
             vm(CHUNKS, CELLS, F),
-            sems(BLOCKS + 1, 2),
+            sems(2 * BLOCKS, 2),
             sems(BLOCKS, 2, GROUP),
             sems(2, GROUP),
-            sems(2, 2, LINE),
-            sems(2, GROUP),
+            sems(BLOCKS, 2, LINE),
+            sems(BLOCKS, 2, GROUP),
             sems(len(arguments)),
             vm(ROWS, COLS, C, dtype=half),
             vm(ROWS, COLS, C, dtype=half),
-            sems(3),
+            sems(4),
             *(pltpu.VMEM(array.shape, array.dtype) for array in arguments),
         ],
         compiler_params=pltpu.CompilerParams(
@@ -766,7 +778,7 @@
             row,
             row,
         ),
-        in_specs=[anywhere, anywhere, vmem],
+        in_specs=[anywhere, anywhere, vmem, vmem],
         out_specs=(anywhere, anywhere) + (vmem,) * 9,
         scratch_shapes=[
             vm(GROUP, 8, C),

time: 81.6 us -> 76.1 us (0.933)
  Pallas kernels: 80.7 us -> 75.3 us
    pallas_call x1, Pallas kernels: 76.9 us -> 71.5 us  [on_device(): pl.pallas_call(step_kernel, name='ocean_step', out_shape=(field, field, j...]
where the time goes in v3:
time: 76.1 us; the launch traced here: 76 us
  Pallas kernels  75.3 us (99%)
    pallas_call x1, Pallas kernels, on_device(): pl.pallas_call(step_kernel, name='ocean_step', out_shape=(field, field, j...  71.5 us
    pallas_call x1, Pallas kernels, on_device(): pl.pallas_call(lambda *refs: write_kernel(grad_norm, *refs), name='write_...  3.84 us

profile of v3, /device:TPU:1, one launch (start us, length us, event | category | flops | bytes accessed | tf_op | source)
XLA Modules:
  0.0 76.0 jit_solution(2192722423065814536)
XLA Ops:
  0.6 71.5 %ocean_step.1 = (bf16[45,24,128]{2,1,0:T(8,128)(2,1)}, bf16[45,24,128]{2,1,0:T(8,128)(2,1)}, bf16[2,16,40,128]{3,2,1,0:T(8,128)(2,1)}, bf16[2,16,32,128]{3,2,1,0:T(8,128)(2,1)}) custom-call(bf16[45,24,128]{2,1,0:T(8,128)(2,1)} %refs_0_.1, s32[24,45]{1,0:T(8,128)} %bitcast.4, bf16[45,24,128]{2,1,0:T(8,128)(2,1)} %refs_2_.1, bf16[7,7,2,128]{3,2,1,0:T(2,128)(2,1)} %bitcast.3, ...), custom_call_target="tpu_custom_call" | custom-call | tf_op jit(solution)/shard_map/ocean_step/pallas_call | solution.py:698
  72.1 3.8 %write_results.1 = (bf16[45,24,128]{2,1,0:T(8,128)(2,1)}, bf16[45,24,128]{2,1,0:T(8,128)(2,1)}, f32[7,7,2,128]{3,2,1,0:T(2,128)}, f32[2,128]{1,0:T(2,128)}, f32[...) custom-call(bf16[45,24,128]{2,1,0:T(8,128)(2,1)} %get-tuple-element., ...), custom_call_target="tpu_custom_call" | custom-call | tf_op jit(solution)/shard_map/write_results/pallas_call | solution.py:765

commit v4 on v3

--- a/solution.py
+++ b/solution.py
@@ -73,40 +73,29 @@
         self.src, self.dst, self.sems = src, dst, sems
         self.me, self.size = (self.plane, GROUP) if kind == "plane" else (self.z, LINE)
 
-    def copy(self, k, arriving):
-        other = lax.rem(self.me + k, self.size)
-        if self.kind == "plane":
-            target = device(other, self.z, self.core)
-        else:
-            target = device(self.plane, other, self.core)
-        if self.scatter:
-            src, slot = self.src.at[other], k
-        else:
-            src = self.src
-            slot = lax.rem(self.me - k + self.size, self.size) if arriving else self.me
-        return pltpu.make_async_remote_copy(
-            src_ref=src,
-            dst_ref=self.dst.at[slot],
-            send_sem=self.sems.at[0, k],
-            recv_sem=self.sems.at[1, k],
-            device_id=target,
-            device_id_type=MESH_ID,
-        )
-
     def start(self):
-        def one(k, carry):
-            self.copy(k, False).start()
-            return carry
-
-        lax.fori_loop(1, self.size, one, 0)
+        for k in range(1, self.size):
+            other = lax.rem(self.me + k, self.size)
+            if self.kind == "plane":
+                target = device(other, self.z, self.core)
+            else:
+                target = device(self.plane, other, self.core)
+            pltpu.make_async_remote_copy(
+                src_ref=self.src.at[other] if self.scatter else self.src,
+                dst_ref=self.dst.at[k if self.scatter else self.me],
+                send_sem=self.sems.at[0],
+                recv_sem=self.sems.at[1],
+                device_id=target,
+                device_id_type=MESH_ID,
+            ).start()
         return self
 
     def wait(self):
-        def one(k, carry):
-            self.copy(k, True).wait()
-            return carry
-
-        lax.fori_loop(1, self.size, one, 0)
+        others = pl.ds(1, self.size - 1)
+        for side in range(2):
+            pltpu.make_async_copy(
+                self.dst.at[others], self.dst.at[others], self.sems.at[side]
+            ).wait()
 
 
 def to_sibling(src, dst, sems):
@@ -385,7 +374,7 @@
             slope[keep, rows, :] = cumulative + h * density
             return carry
 
-        lax.fori_loop(0, STRIP, gelu, 0)
+        lax.fori_loop(0, STRIP, gelu, 0, unroll=3)
         act = active[keep]
         branch_c = (
             jnp.dot(act, weight_out[blk], preferred_element_type=jnp.float32)
@@ -616,8 +605,8 @@
     grad_norm,
     out_from,
     state_from,
-    sums_one,
-    sums_two,
+    one_from,
+    two_from,
     out,
     grad_state,
     g_kernel,
@@ -631,26 +620,40 @@
     g_scale,
     small,
     held,
+    sums_one,
+    sums_two,
+    win,
+    wout,
     sems,
 ):
-    pairs = ((out_from, out), (state_from, grad_state))
-    moves = [
-        pltpu.make_async_copy(pair[0], held.at[n], sems.at[n]) for n, pair in enumerate(pairs)
-    ]
-    for move in moves:
-        move.start()
-    for n, pair in enumerate(pairs):
-        moves[n].wait()
-        moves[n] = pltpu.make_async_copy(held.at[n], pair[1], sems.at[2 + n])
-        moves[n].start()
-    for blk in range(BLOCKS):
-        sums = (sums_one, sums_two)[blk]
+    def move(source, target, n):
+        copy = pltpu.make_async_copy(source, target, sems.at[n])
+        copy.start()
+        return copy
+
+    two_in = move(two_from, sums_two, 0)
+    fields_in = [move(out_from, held.at[0], 1), move(state_from, held.at[1], 2)]
+    one_in = move(one_from, sums_one, 3)
+    leaving = []
+
+    def widen(blk, sums):
         rows = slice(0, PIECE)
         for p in range(GROUP):
-            g_win[
+            win[
                 blk, (p % 4) * PIECE : (p % 4) * PIECE + PIECE, (p // 4) * 128 : (p // 4) * 128 + 128
             ] = f32(sums[0, p, rows, :]) * grad_norm
-            g_wout[blk, p * PIECE : p * PIECE + PIECE] = f32(sums[1, p, rows, :]) * grad_norm
+            wout[blk, p * PIECE : p * PIECE + PIECE] = f32(sums[1, p, rows, :]) * grad_norm
+        leaving.append(move(win.at[blk], g_win.at[blk], 4 + 2 * blk))
+        leaving.append(move(wout.at[blk], g_wout.at[blk], 5 + 2 * blk))
+
+    two_in.wait()
+    widen(1, sums_two)
+    fields_in[0].wait()
+    leaving.append(move(held.at[0], out, 8))
+    fields_in[1].wait()
+    leaving.append(move(held.at[1], grad_state, 9))
+    one_in.wait()
+    widen(0, sums_one)
     tiny = slice(PIECE, PIECE + 8)
     for p in range(GROUP):
         small[p] = (f32(sums_one[0, p, tiny, :]) + f32(sums_one[1, p, tiny, :])) * grad_norm
@@ -666,8 +669,8 @@
             ref[blk : blk + 1, :] = row_of(49 + k)
         for q in range(4):
             g_bias_in[blk : blk + 1, q * 128 : q * 128 + 128] = row_of(54 + q)
-    for move in moves:
-        move.wait()
+    for copy in leaving:
+        copy.wait()
 
 
 def on_device(
@@ -748,10 +751,10 @@
             vm(CHUNKS, CELLS, C, dtype=half),
             vm(CHUNKS, CELLS, F),
             sems(2 * BLOCKS, 2),
-            sems(BLOCKS, 2, GROUP),
-            sems(2, GROUP),
-            sems(BLOCKS, 2, LINE),
-            sems(BLOCKS, 2, GROUP),
+            sems(BLOCKS, 2),
+            sems(2),
+            sems(BLOCKS, 2),
+            sems(BLOCKS, 2),
             sems(len(arguments)),
             vm(ROWS, COLS, C, dtype=half),
             vm(ROWS, COLS, C, dtype=half),
@@ -778,12 +781,16 @@
             row,
             row,
         ),
-        in_specs=[anywhere, anywhere, vmem, vmem],
-        out_specs=(anywhere, anywhere) + (vmem,) * 9,
+        in_specs=[anywhere] * 4,
+        out_specs=(anywhere, anywhere, vmem, vmem, vmem, vmem, anywhere, vmem, anywhere, vmem, vmem),
         scratch_shapes=[
             vm(GROUP, 8, C),
             vm(2, ROWS, COLS, C, dtype=half),
-            sems(4),
+            vm(2, GROUP, packed, C, dtype=half),
+            vm(2, GROUP, PIECE, C, dtype=half),
+            vm(BLOCKS, C, F),
+            vm(BLOCKS, F, C),
+            sems(10),
         ],
         compiler_params=pltpu.CompilerParams(vmem_limit_bytes=58 << 20),
     )(*fields)

time: 76.1 us -> 71.3 us (0.937)
  Pallas kernels: 75.3 us -> 70.6 us
    pallas_call x1, Pallas kernels: 71.5 us -> 67.7 us  [on_device(): pl.pallas_call(step_kernel, name='ocean_step', out_shape=(field, field, j...]
    pallas_call x1, Pallas kernels: 3.84 us -> 2.86 us  [on_device(): pl.pallas_call(lambda *refs: write_kernel(grad_norm, *refs), name='write_...]
where the time goes in v4:
time: 71.3 us; the launch traced here: 71.2 us
  Pallas kernels  70.6 us (99%)
    pallas_call x1, Pallas kernels, on_device(): pl.pallas_call(step_kernel, name='ocean_step', out_shape=(field, field, j...  67.7 us
    pallas_call x1, Pallas kernels, on_device(): pl.pallas_call(lambda *refs: write_kernel(grad_norm, *refs), name='write_...  2.86 us

profile of v4, /device:TPU:1, one launch (start us, length us, event | category | flops | bytes accessed | tf_op | source)
XLA Modules:
  0.0 71.2 jit_solution(1882144033448012652)
XLA Ops:
  0.6 67.7 %ocean_step.1 = (bf16[45,24,128]{2,1,0:T(8,128)(2,1)}, bf16[45,24,128]{2,1,0:T(8,128)(2,1)}, bf16[2,16,40,128]{3,2,1,0:T(8,128)(2,1)}, bf16[2,16,32,128]{3,2,1,0:T(8,128)(2,1)}) custom-call(bf16[45,24,128]{2,1,0:T(8,128)(2,1)} %refs_0_.1, s32[24,45]{1,0:T(8,128)} %bitcast.4, bf16[45,24,128]{2,1,0:T(8,128)(2,1)} %refs_2_.1, bf16[7,7,2,128]{3,2,1,0:T(2,128)(2,1)} %bitcast.3, ...), custom_call_target="tpu_custom_call" | custom-call | tf_op jit(solution)/shard_map/ocean_step/pallas_call | solution.py:701
  68.4 2.9 %write_results.1 = (bf16[45,24,128]{2,1,0:T(8,128)(2,1)}, bf16[45,24,128]{2,1,0:T(8,128)(2,1)}, f32[7,7,2,128]{3,2,1,0:T(2,128)}, f32[2,128]{1,0:T(2,128)}, f32[...) custom-call(bf16[45,24,128]{2,1,0:T(8,128)(2,1)} %get-tuple-element., ...), custom_call_target="tpu_custom_call" | custom-call | tf_op jit(solution)/shard_map/write_results/pallas_call | solution.py:768

commit v5 on v4

--- a/solution.py
+++ b/solution.py
@@ -22,7 +22,7 @@
 COLS = 24
 MARGIN = 3
 AROUND = ((1, 0), (-1, 0), (0, 1), (0, -1), (1, 1), (1, -1), (-1, 1), (-1, -1))
-STRIP = 9
+STRIP = 15
 CHUNKS = ROWS // STRIP
 CELLS = STRIP * COLS
 
@@ -207,10 +207,10 @@
 def convolve(window, weight, first, flip):
     def rows(base):
         sums = first(base)
-        for i in range(KSIZE + 2):
+        for i in range(KSIZE + 4):
             for b in range(KSIZE):
                 piece = window[base + i, b : b + COLS, :]
-                for o in range(3):
+                for o in range(5):
                     a = i - o
                     if 0 <= a < KSIZE:
                         tap = weight(KSIZE - 1 - a, KSIZE - 1 - b) if flip else weight(a, b)
@@ -344,16 +344,16 @@
     def mix(window, blk):
         start = jnp.broadcast_to(conv_bias[blk : blk + 1, :], (COLS, C))
         rows = convolve(
-            window, lambda a, b: taps[a, b, blk : blk + 1, :], lambda base: [start] * 3, False
-        )
-
-        def three(g, carry):
-            sums = rows(g * 3)
-            for o in range(3):
-                mixed[g * 3 + o] = sums[o]
+            window, lambda a, b: taps[a, b, blk : blk + 1, :], lambda base: [start] * 5, False
+        )
+
+        def five(g, carry):
+            sums = rows(g * 5)
+            for o in range(5):
+                mixed[g * 5 + o] = sums[o]
             return carry
 
-        lax.fori_loop(0, ROWS // 3, three, 0)
+        lax.fori_loop(0, ROWS // 5, five, 0)
 
     def forward(c, window, blk, keep):
         x = mixed[pl.ds(c * STRIP, STRIP)].reshape(CELLS, C)
@@ -374,7 +374,7 @@
             slope[keep, rows, :] = cumulative + h * density
             return carry
 
-        lax.fori_loop(0, STRIP, gelu, 0, unroll=3)
+        lax.fori_loop(0, STRIP, gelu, 0, unroll=15)
         act = active[keep]
         branch_c = (
             jnp.dot(act, weight_out[blk], preferred_element_type=jnp.float32)
@@ -447,17 +447,17 @@
         rows = convolve(
             gwindow,
             lambda a, b: taps[a, b, blk : blk + 1, :],
-            lambda base: [upstream[base + o] for o in range(3)],
+            lambda base: [upstream[base + o] for o in range(5)],
             True,
         )
 
-        def three(g, carry):
-            sums = rows(g * 3)
-            for o in range(3):
-                put(g * 3 + o, sums[o])
+        def five(g, carry):
+            sums = rows(g * 5)
+            for o in range(5):
+                put(g * 5 + o, sums[o])
             return carry
 
-        lax.fori_loop(begin, end, three, 0)
+        lax.fori_loop(begin, end, five, 0)
 
     def core_sum(blk):
         for q in range(4):
@@ -560,7 +560,7 @@
     def put_mixed(row, value):
         mixed[row] = f32(bf16(value))
 
-    adjoint(gwin2, 1, put_mixed, 0, 15)
+    adjoint(gwin2, 1, put_mixed, 0, 9)
     second = line_sum(second, 1, None)
 
     def backward_one(c, carry):
@@ -572,21 +572,21 @@
     halo = Halo(halo_bufs, sem_h, 3, gwin1)
     halo.start()
     first = core_sum(0)
-    second = plane_back(second, 1, gather_two)
     tap_sums(win1, gwin1, 0, 0, 6)
     first = plane_sum(first, 0)
     tap_sums(win1, gwin1, 0, 6, 15)
     pack_rows(0)
     tiny = Exchange("plane", True, small, tiny_a, sem_tiny).start()
-    second = swap_halves(second, 1, gather_two)
+    second = plane_back(second, 1, gather_two)
     halo.finish()
 
     def put_state(row, value):
         grad_state[row] = bf16(value)
 
-    adjoint(gwin1, 0, put_state, 0, 8)
+    adjoint(gwin1, 0, put_state, 0, 5)
     first = line_sum(first, 0, tiny)
-    adjoint(gwin1, 0, put_state, 8, 15)
+    second = swap_halves(second, 1, gather_two)
+    adjoint(gwin1, 0, put_state, 5, 9)
     put_grad = pltpu.make_async_copy(grad_state, state_hbm, sem_put.at[1])
     put_grad.start()
     second.wait()

time: 71.3 us -> 66.3 us (0.930)
  Pallas kernels: 70.6 us -> 65.5 us
    pallas_call x1, Pallas kernels: 67.7 us -> 62.6 us  [on_device(): pl.pallas_call(step_kernel, name='ocean_step', out_shape=(field, field, j...]
where the time goes in v5:
time: 66.3 us; the launch traced here: 66.1 us
  Pallas kernels  65.5 us (99%)
    pallas_call x1, Pallas kernels, on_device(): pl.pallas_call(step_kernel, name='ocean_step', out_shape=(field, field, j...  62.6 us
    pallas_call x1, Pallas kernels, on_device(): pl.pallas_call(lambda *refs: write_kernel(grad_norm, *refs), name='write_...  2.86 us

profile of v5, /device:TPU:1, one launch (start us, length us, event | category | flops | bytes accessed | tf_op | source)
XLA Modules:
  0.0 66.1 jit_solution(7730051425416533057)
XLA Ops:
  0.6 62.6 %ocean_step.1 = (bf16[45,24,128]{2,1,0:T(8,128)(2,1)}, bf16[45,24,128]{2,1,0:T(8,128)(2,1)}, bf16[2,16,40,128]{3,2,1,0:T(8,128)(2,1)}, bf16[2,16,32,128]{3,2,1,0:T(8,128)(2,1)}) custom-call(bf16[45,24,128]{2,1,0:T(8,128)(2,1)} %refs_0_.1, s32[24,45]{1,0:T(8,128)} %bitcast.4, bf16[45,24,128]{2,1,0:T(8,128)(2,1)} %refs_2_.1, bf16[7,7,2,128]{3,2,1,0:T(2,128)(2,1)} %bitcast.3, ...), custom_call_target="tpu_custom_call" | custom-call | tf_op jit(solution)/shard_map/ocean_step/pallas_call | solution.py:701
  63.3 2.9 %write_results.1 = (bf16[45,24,128]{2,1,0:T(8,128)(2,1)}, bf16[45,24,128]{2,1,0:T(8,128)(2,1)}, f32[7,7,2,128]{3,2,1,0:T(2,128)}, f32[2,128]{1,0:T(2,128)}, f32[...) custom-call(bf16[45,24,128]{2,1,0:T(8,128)(2,1)} %get-tuple-element., ...), custom_call_target="tpu_custom_call" | custom-call | tf_op jit(solution)/shard_map/write_results/pallas_call | solution.py:768

commit v6 on v5

--- a/solution.py
+++ b/solution.py
@@ -127,9 +127,10 @@
 
 class Halo:
     def __init__(self, bufs, sems, index, window):
-        east, west, north, south, from_west, from_east, from_north, from_south = (
-            ref.at[index] for ref in bufs
-        )
+        east, west, north, south, self.sides, self.ends = (ref.at[index] for ref in bufs)
+        from_west, from_east = self.sides.at[0], self.sides.at[1]
+        from_north, from_south = self.ends.at[0], self.ends.at[1]
+        self.sems = sems.at[index]
         self.bufs = (east, west, north, south, from_west, from_east, from_north, from_south)
         self.window = window
         last = ROWS - MARGIN
@@ -150,8 +151,8 @@
             pltpu.make_async_remote_copy(
                 src_ref=pair[0],
                 dst_ref=pair[1],
-                send_sem=sems.at[index, 0, k],
-                recv_sem=sems.at[index, 1, k],
+                send_sem=sems.at[index, 0, int(k in (2, 3))],
+                recv_sem=sems.at[index, 1, int(k in (2, 3))],
                 device_id=beside(*AROUND[k]),
                 device_id_type=MESH_ID,
             )
@@ -183,8 +184,9 @@
             copy.start()
 
     def finish(self):
-        for copy in self.copies:
-            copy.wait()
+        for kind, ref in enumerate((self.sides, self.ends)):
+            for side in range(2):
+                pltpu.make_async_copy(ref, ref, self.sems.at[side, kind]).wait()
         from_west, from_east, from_north, from_south = self.bufs[4:]
         lat = lax.axis_index("lat")
         has_north = jnp.where(lat > 0, 1.0, 0.0).astype(jnp.float32)
@@ -260,10 +262,8 @@
     h_west,
     h_north,
     h_south,
-    h_from_west,
-    h_from_east,
-    h_from_north,
-    h_from_south,
+    h_sides,
+    h_ends,
     sem_h,
     small,
     halves,
@@ -313,7 +313,7 @@
     announce(barrier)
     loads[0].wait()
     halo_bufs = (
-        h_east, h_west, h_north, h_south, h_from_west, h_from_east, h_from_north, h_from_south
+        h_east, h_west, h_north, h_south, h_sides, h_ends
     )
     middle = slice(MARGIN, MARGIN + COLS)
 
@@ -425,14 +425,14 @@
         gwindow[pl.ds(MARGIN + c * STRIP, STRIP), middle, :] = gm.reshape(STRIP, COLS, C)
 
     def tap_sums(window, gwindow, blk, begin, end):
-        def three(g, carry):
-            base = g * 3
-            grads = [gwindow[base + MARGIN + o, middle, :] for o in range(3)]
+        def five(g, carry):
+            base = g * 5
+            grads = [gwindow[base + MARGIN + o, middle, :] for o in range(5)]
             for b in range(KSIZE):
                 parts = [None] * KSIZE
-                for i in range(KSIZE + 2):
+                for i in range(KSIZE + 4):
                     piece = window[base + i, b : b + COLS, :]
-                    for o in range(3):
+                    for o in range(5):
                         a = i - o
                         if 0 <= a < KSIZE:
                             term = piece * grads[o]
@@ -441,7 +441,7 @@
                     acc_taps[blk, a * KSIZE + b] += fold(parts[a])
             return carry
 
-        lax.fori_loop(begin, end, three, 0)
+        lax.fori_loop(begin, end, five, 0)
 
     def adjoint(gwindow, blk, put, begin, end):
         rows = convolve(
@@ -528,7 +528,7 @@
         )
         return carry
 
-    lax.fori_loop(0, CHUNKS, forward_one, 0)
+    lax.fori_loop(0, CHUNKS, forward_one, 0, unroll=True)
     halo = Halo(halo_bufs, sem_h, 1, win2)
     halo.start()
 
@@ -536,7 +536,7 @@
         seed(c, f32(cotangent[pl.ds(c * STRIP, STRIP)]).reshape(CELLS, C), 1)
         return carry
 
-    lax.fori_loop(0, CHUNKS, seed_two, 0)
+    lax.fori_loop(0, CHUNKS, seed_two, 0, unroll=True)
     halo.finish()
     mix(win2, 1)
 
@@ -546,13 +546,13 @@
         backward(c, gwin2, 1, CHUNKS)
         return carry
 
-    lax.fori_loop(0, CHUNKS, both, 0)
+    lax.fori_loop(0, CHUNKS, both, 0, unroll=True)
     put_out = pltpu.make_async_copy(out, out_hbm, sem_put.at[0])
     put_out.start()
     halo = Halo(halo_bufs, sem_h, 2, gwin2)
     halo.start()
     second = core_sum(1)
-    tap_sums(win2, gwin2, 1, 0, 15)
+    tap_sums(win2, gwin2, 1, 0, 9)
     second = plane_sum(second, 1)
     pack_rows(1)
     halo.finish()
@@ -568,13 +568,13 @@
         backward(c, gwin1, 0, c)
         return carry
 
-    lax.fori_loop(0, CHUNKS, backward_one, 0)
+    lax.fori_loop(0, CHUNKS, backward_one, 0, unroll=True)
     halo = Halo(halo_bufs, sem_h, 3, gwin1)
     halo.start()
     first = core_sum(0)
-    tap_sums(win1, gwin1, 0, 0, 6)
+    tap_sums(win1, gwin1, 0, 0, 4)
     first = plane_sum(first, 0)
-    tap_sums(win1, gwin1, 0, 6, 15)
+    tap_sums(win1, gwin1, 0, 4, 9)
     pack_rows(0)
     tiny = Exchange("plane", True, small, tiny_a, sem_tiny).start()
     second = plane_back(second, 1, gather_two)
@@ -733,11 +733,9 @@
             vm(4, ROWS, MARGIN, C, dtype=half),
             vm(4, MARGIN, COLS, C, dtype=half),
             vm(4, MARGIN, COLS, C, dtype=half),
-            vm(4, tall, MARGIN, C, dtype=half),
-            vm(4, tall, MARGIN, C, dtype=half),
-            vm(4, MARGIN, COLS, C, dtype=half),
-            vm(4, MARGIN, COLS, C, dtype=half),
-            sems(4, 2, len(AROUND)),
+            vm(4, 2, tall, MARGIN, C, dtype=half),
+            vm(4, 2, MARGIN, COLS, C, dtype=half),
+            sems(4, 2, 2),
             vm(GROUP, 8, C),
             vm(BLOCKS, 2, F, C, dtype=half),
             vm(BLOCKS, F, C, dtype=half),

time: 66.3 us -> 63.6 us (0.959)
  Pallas kernels: 65.5 us -> 62.8 us
    pallas_call x1, Pallas kernels: 62.6 us -> 59.9 us  [on_device(): pl.pallas_call(step_kernel, name='ocean_step', out_shape=(field, field, j...]
where the time goes in v6:
time: 63.6 us; the launch traced here: 63.4 us
  Pallas kernels  62.8 us (99%)
  between operations  0.66 us (1%)
    pallas_call x1, Pallas kernels, on_device(): pl.pallas_call(step_kernel, name='ocean_step', out_shape=(field, field, j...  59.9 us
    pallas_call x1, Pallas kernels, on_device(): pl.pallas_call(lambda *refs: write_kernel(grad_norm, *refs), name='write_...  2.86 us

profile of v6, /device:TPU:1, one launch (start us, length us, event | category | flops | bytes accessed | tf_op | source)
XLA Modules:
  0.0 63.4 jit_solution(1944110222864809259)
XLA Ops:
  0.6 59.9 %ocean_step.1 = (bf16[45,24,128]{2,1,0:T(8,128)(2,1)}, bf16[45,24,128]{2,1,0:T(8,128)(2,1)}, bf16[2,16,40,128]{3,2,1,0:T(8,128)(2,1)}, bf16[2,16,32,128]{3,2,1,0:T(8,128)(2,1)}) custom-call(bf16[45,24,128]{2,1,0:T(8,128)(2,1)} %refs_0_.1, s32[24,45]{1,0:T(8,128)} %bitcast.4, bf16[45,24,128]{2,1,0:T(8,128)(2,1)} %refs_2_.1, bf16[7,7,2,128]{3,2,1,0:T(2,128)(2,1)} %bitcast.3, ...), custom_call_target="tpu_custom_call" | custom-call | tf_op jit(solution)/shard_map/ocean_step/pallas_call | solution.py:701
  60.6 2.9 %write_results.1 = (bf16[45,24,128]{2,1,0:T(8,128)(2,1)}, bf16[45,24,128]{2,1,0:T(8,128)(2,1)}, f32[7,7,2,128]{3,2,1,0:T(2,128)}, f32[2,128]{1,0:T(2,128)}, f32[...) custom-call(bf16[45,24,128]{2,1,0:T(8,128)(2,1)} %get-tuple-element., ...), custom_call_target="tpu_custom_call" | custom-call | tf_op jit(solution)/shard_map/write_results/pallas_call | solution.py:766

commit v7 on v6

--- a/solution.py
+++ b/solution.py
@@ -62,8 +62,10 @@
         signal(device(plane, lax.rem(z + k, LINE), core))
         return carry
 
-    lax.fori_loop(1, GROUP, in_plane, 0)
-    lax.fori_loop(1, LINE, in_line, 0)
+    for k in range(1, GROUP):
+        in_plane(k, 0)
+    for k in range(1, LINE):
+        in_line(k, 0)
 
 
 class Exchange:
@@ -353,7 +355,7 @@
                 mixed[g * 5 + o] = sums[o]
             return carry
 
-        lax.fori_loop(0, ROWS // 5, five, 0)
+        lax.fori_loop(0, ROWS // 5, five, 0, unroll=3)
 
     def forward(c, window, blk, keep):
         x = mixed[pl.ds(c * STRIP, STRIP)].reshape(CELLS, C)

time: 63.6 us -> 63.3 us (level)
  no operation moved by 1% of the time
where the time goes in v7:
time: 63.3 us; the launch traced here: 63.2 us
  Pallas kernels  62.5 us (99%)
  between operations  0.66 us (1%)
    pallas_call x1, Pallas kernels, on_device(): pl.pallas_call(step_kernel, name='ocean_step', out_shape=(field, field, j...  59.7 us
    pallas_call x1, Pallas kernels, on_device(): pl.pallas_call(lambda *refs: write_kernel(grad_norm, *refs), name='write_...  2.86 us

profile of v7, /device:TPU:1, one launch (start us, length us, event | category | flops | bytes accessed | tf_op | source)
XLA Modules:
  0.0 63.2 jit_solution(17750124481921001374)
XLA Ops:
  0.6 59.7 %ocean_step.1 = (bf16[45,24,128]{2,1,0:T(8,128)(2,1)}, bf16[45,24,128]{2,1,0:T(8,128)(2,1)}, bf16[2,16,40,128]{3,2,1,0:T(8,128)(2,1)}, bf16[2,16,32,128]{3,2,1,0:T(8,128)(2,1)}) custom-call(bf16[45,24,128]{2,1,0:T(8,128)(2,1)} %refs_0_.1, s32[24,45]{1,0:T(8,128)} %bitcast.4, bf16[45,24,128]{2,1,0:T(8,128)(2,1)} %refs_2_.1, bf16[7,7,2,128]{3,2,1,0:T(2,128)(2,1)} %bitcast.3, ...), custom_call_target="tpu_custom_call" | custom-call | tf_op jit(solution)/shard_map/ocean_step/pallas_call | solution.py:703
  60.3 2.9 %write_results.1 = (bf16[45,24,128]{2,1,0:T(8,128)(2,1)}, bf16[45,24,128]{2,1,0:T(8,128)(2,1)}, f32[7,7,2,128]{3,2,1,0:T(2,128)}, f32[2,128]{1,0:T(2,128)}, f32[...) custom-call(bf16[45,24,128]{2,1,0:T(8,128)(2,1)} %get-tuple-element., ...), custom_call_target="tpu_custom_call" | custom-call | tf_op jit(solution)/shard_map/write_results/pallas_call | solution.py:768

commit v8 on v7

--- a/solution.py
+++ b/solution.py
@@ -365,11 +365,11 @@
         normed[keep] = norm
         inverse[keep] = jnp.broadcast_to(inv, (CELLS, C))
         lifted = bf16(norm * norm_gain[blk : blk + 1, :] + norm_bias[blk : blk + 1, :])
-        hidden[...] = jnp.dot(lifted, weight_in[blk], preferred_element_type=jnp.float32)
+        hidden[keep] = jnp.dot(lifted, weight_in[blk], preferred_element_type=jnp.float32)
 
         def gelu(t, carry):
             rows = pl.ds(pl.multiple_of(t * COLS, 8), COLS)
-            h = hidden[rows, :] + bias_in[blk : blk + 1, :]
+            h = hidden[keep, rows, :] + bias_in[blk : blk + 1, :]
             cumulative = 0.5 * (1.0 + lax.erf(h * INV_ROOT_TWO))
             density = jnp.exp(-0.5 * h * h) * INV_ROOT_TWO_PI
             active[keep, rows, :] = bf16(h * cumulative)
@@ -543,9 +543,9 @@
     mix(win2, 1)
 
     def both(c, carry):
-        result = forward(c, win2, 1, CHUNKS)
+        result = forward(c, win2, 1, CHUNKS + c)
         out[pl.ds(c * STRIP, STRIP)] = bf16(result.reshape(STRIP, COLS, C))
-        backward(c, gwin2, 1, CHUNKS)
+        backward(c, gwin2, 1, CHUNKS + c)
         return carry
 
     lax.fori_loop(0, CHUNKS, both, 0, unroll=True)
@@ -719,12 +719,12 @@
             vm(KSIZE, KSIZE, BLOCKS, C),
             vm(ROWS, COLS, C),
             vm(ROWS, COLS, C),
-            vm(CELLS, F),
-            vm(CHUNKS + 1, CELLS, F, dtype=half),
-            vm(CHUNKS + 1, CELLS, F),
-            vm(CHUNKS + 1, CELLS, C),
-            vm(CHUNKS + 1, CELLS, C),
-            vm(CHUNKS + 1, CELLS, C),
+            vm(2 * CHUNKS, CELLS, F),
+            vm(2 * CHUNKS, CELLS, F, dtype=half),
+            vm(2 * CHUNKS, CELLS, F),
+            vm(2 * CHUNKS, CELLS, C),
+            vm(2 * CHUNKS, CELLS, C),
+            vm(2 * CHUNKS, CELLS, C),
             vm(ROWS, COLS, C),
             vm(BLOCKS, C, F),
             vm(BLOCKS, C, F),

time: 63.3 us -> 63.3 us (level)
  no operation moved by 1% of the time
where the time goes in v8:
time: 63.3 us; the launch traced here: 63.1 us
  Pallas kernels  62.5 us (99%)
  between operations  0.66 us (1%)
    pallas_call x1, Pallas kernels, on_device(): pl.pallas_call(step_kernel, name='ocean_step', out_shape=(field, field, j...  59.6 us
    pallas_call x1, Pallas kernels, on_device(): pl.pallas_call(lambda *refs: write_kernel(grad_norm, *refs), name='write_...  2.86 us

profile of v8, /device:TPU:1, one launch (start us, length us, event | category | flops | bytes accessed | tf_op | source)
XLA Modules:
  0.0 63.1 jit_solution(6814400093848558156)
XLA Ops:
  0.6 59.6 %ocean_step.1 = (bf16[45,24,128]{2,1,0:T(8,128)(2,1)}, bf16[45,24,128]{2,1,0:T(8,128)(2,1)}, bf16[2,16,40,128]{3,2,1,0:T(8,128)(2,1)}, bf16[2,16,32,128]{3,2,1,0:T(8,128)(2,1)}) custom-call(bf16[45,24,128]{2,1,0:T(8,128)(2,1)} %refs_0_.1, s32[24,45]{1,0:T(8,128)} %bitcast.4, bf16[45,24,128]{2,1,0:T(8,128)(2,1)} %refs_2_.1, bf16[7,7,2,128]{3,2,1,0:T(2,128)(2,1)} %bitcast.3, ...), custom_call_target="tpu_custom_call" | custom-call | tf_op jit(solution)/shard_map/ocean_step/pallas_call | solution.py:703
  60.3 2.9 %write_results.1 = (bf16[45,24,128]{2,1,0:T(8,128)(2,1)}, bf16[45,24,128]{2,1,0:T(8,128)(2,1)}, f32[7,7,2,128]{3,2,1,0:T(2,128)}, f32[2,128]{1,0:T(2,128)}, f32[...) custom-call(bf16[45,24,128]{2,1,0:T(8,128)(2,1)} %get-tuple-element., ...), custom_call_target="tpu_custom_call" | custom-call | tf_op jit(solution)/shard_map/write_results/pallas_call | solution.py:768
